TPU v7x, 128 devices: a whole 4x4x4 slice. The times are simulated.
128 devices in a mesh: dp: 8 (over y, core), tensor: 16 (over z, x).
Axes of the slice: x: 4, y: 4, z: 4, core: 2. Of those that a mesh axis runs over, the one named last changes fastest.
Arguments:
- query_weight: bfloat16 [1536, 12288], P(('dp', 'tensor')), may hold values from -6 to 6
- query_state: float32 [1536, 12288], P(('dp', 'tensor')), may hold values from -6 to 6
- latent_weight: bfloat16 [512, 16384], P(('dp', 'tensor')), may hold values from -6 to 6
- latent_state: float32 [512, 16384], P(('dp', 'tensor')), may hold values from -6 to 6
- expert_weight: bfloat16 [16, 7168, 2048], P('tensor', 'dp'), may hold values from -6 to 6
- expert_state: float32 [16, 7168, 2048], P('tensor', 'dp'), may hold values from -6 to 6
- decay: float32 [3], replicated, may hold values from 0.5 to 0.9
- shard_expert: int32 [16], replicated, may hold values from 0 to 15, each once
- host_slots: int32 [16, 2], replicated, may hold values from -1 to 15, as said below
Outputs:
- query_serving: bfloat16 [1536, 12288], P(None, 'tensor')
- latent_serving: bfloat16 [512, 16384], P(None, 'tensor')
- expert_serving: bfloat16 [16, 2, 7168, 2048], P('tensor', None, 'dp')
Inputs may be any that keep to these rules, and one draw needn't show every extreme that they name: `shard_expert`: a permutation: each expert is held by exactly one trainer shard. `host_slots`: each row lists the experts of one host; no expert twice in a row; every expert appears in some row; some slots are empty.
All inputs are finite; a program needn't handle non-finite values.
Results may differ from a plain program's by a relative error of at most 0.001.
Values may be sent and summed in bfloat16 or wider, within the bound.
A program may use at most 320 MiB of HBM per device.

v0:
```python
import jax
import jax.numpy as jnp
from jax import lax
from jax.sharding import PartitionSpec as P


def publish(weight_part, state_part, rate):
    return (rate * state_part + (1.0 - rate) * weight_part.astype(jnp.float32)).astype(jnp.bfloat16)


def regroup(moved, host_count, groups):
    block_rows = moved.shape[0] // (host_count * groups)
    shaped = moved.reshape(host_count, groups, block_rows, moved.shape[1])
    return shaped.transpose(1, 0, 2, 3).reshape(groups * host_count * block_rows, moved.shape[1])


def per_device(
    query_weight,
    query_state,
    latent_weight,
    latent_state,
    expert_weight,
    expert_state,
    decay,
    shard_expert,
    host_slots,
):
    host_count = lax.axis_size("tensor")
    groups = lax.axis_size("dp")
    query_block = publish(query_weight, query_state, decay[0])
    latent_block = publish(latent_weight, latent_state, decay[1])
    query_rows, latent_rows = (
        lax.all_gather(query_block, "dp", axis=0, tiled=True),
        lax.all_gather(latent_block, "dp", axis=0, tiled=True),
    )
    query_moved, latent_moved = (
        lax.all_to_all(query_rows, "tensor", split_axis=1, concat_axis=0, tiled=True),
        lax.all_to_all(latent_rows, "tensor", split_axis=1, concat_axis=0, tiled=True),
    )
    query_serving = regroup(query_moved, host_count, groups)
    latent_serving = regroup(latent_moved, host_count, groups)
    blended = publish(expert_weight, expert_state, decay[2])
    count = shard_expert.shape[0]
    ids = jnp.arange(count, dtype=jnp.int32)
    inverse = jnp.sum(jnp.where(shard_expert[None, :] == ids[:, None], ids[None, :], 0), axis=1)
    slot_clamped = jnp.maximum(host_slots, 0)
    stored = jnp.sum(
        jnp.where(slot_clamped[:, :, None] == ids[None, None, :], inverse[None, None, :], 0), axis=2
    )
    filled = host_slots >= 0
    position = lax.axis_index("tensor")
    own_expert = jnp.sum(jnp.where(ids == position, shard_expert, 0))
    listed = jnp.any(host_slots == own_expert, axis=1)
    outgoing = jnp.where(listed[:, None, None], blended, jnp.zeros_like(blended))
    received = lax.all_to_all(outgoing, "tensor", split_axis=0, concat_axis=0, tiled=True)
    own_stored = lax.dynamic_index_in_dim(stored, position, 0, keepdims=False)
    own_filled = lax.dynamic_index_in_dim(filled, position, 0, keepdims=False)
    picked = received[own_stored]
    picked = jnp.where(own_filled[:, None, None], picked, jnp.zeros_like(picked))
    expert_serving = picked[None]
    return (query_serving, latent_serving, expert_serving)


def solution(mesh):
    placed = (
        P(("dp", "tensor"), None),
        P(("dp", "tensor"), None),
        P(("dp", "tensor"), None),
        P(("dp", "tensor"), None),
        P("tensor", "dp", None),
        P("tensor", "dp", None),
        P(),
        P(),
        P(),
    )
    return jax.shard_map(
        per_device,
        mesh=mesh,
        in_specs=placed,
        out_specs=(P(None, "tensor"), P(None, "tensor"), P("tensor", None, "dp", None)),
        check_vma=False,
    )
```

profile of v0, /device:TPU:0, one launch (start us, length us, event | category | flops | bytes accessed | tf_op | source)
XLA Modules:
  0.0 1080.8 jit_solution(17235766836861286604)
XLA Ops:
  7.2 0.0 copy-start
  7.2 0.0 all-gather.7.cloned.1.call-start
  7.2 1.4 fusion.7
  9.2 2.4 fusion.3
  11.6 0.0 all-gather.7.cloned.1.call-update
  11.7 0.0 all-gather.5.cloned.1.call-start
  12.4 2.8 fusion.2
  15.1 0.0 all-gather.5.cloned.1.call-update
  15.8 1.3 fusion.4
  17.1 20.5 %all-gather.7.cloned.1.call-done = bf16[8,4,16384]{2,1,0:T(4,128)(2,1)} async-done(((bf16[1,4,16384]{2,1,0:T(4,128)(2,1)}), bf16[8,4,16384]{2,1,0:T(4,128)(2,1)}) %all-gather.7.cloned.1.call-update) | async-done | bytes 1048592 | tf_op jit(solution)/shard_map/all_gather | solution.py:34
  37.6 1.8 all_to_all.30
  39.4 1.5 copy.34
  40.9 6.9 all-to-all-start.1
  47.9 0.0 copy-done
  47.9 0.7 broadcast_compare_fusion
  48.6 8.5 fusion.1
  57.0 10.5 all-gather.5.cloned.1.call-done
  67.5 3.8 all_to_all.27
  71.4 2.1 copy.31
  73.5 0.0 all-to-all-done.1
  73.5 6.9 all-to-all-start
  80.5 21.1 %broadcast_select_fusion = bf16[16,896,2048]{2,1,0:T(8,128)(2,1)} fusion(pred[16]{0:T(512)(128)(4,1)S(1)} %get-tuple-element.6, bf16[896,2048]{1,0:T(8,128)(2,1)} %fusion.1), kind=kLoop, calls=%fused_computation.2 | loop fusion | flops 29360128 | bytes 62390288 | tf_op jit(solution)/shard_map/jit(_where)/select_n | solution.py:54
  101.6 0.0 copy-start.1
  101.6 16.0 %all-to-all-done = bf16[96,16,768]{2,0,1:T(8,128)(2,1)S(1)} async-done(((bf16[96,16,768]{2,0,1:T(8,128)(2,1)}), bf16[96,16,768]{2,0,1:T(8,128)(2,1)S(1)}, u32[]{:S(2)}, u32[]{:S(2)}) %all-to-all-start) | async-done | bytes 2359328 | tf_op jit(solution)/shard_map/all_to_all | solution.py:37
  117.6 7.1 all-to-all-start.2
  124.7 0.0 copy-done.1
  124.7 0.1 select_reduce_fusion.1
  124.9 0.2 select_reduce_fusion
  125.0 0.2 dynamic-slice_reduce_fusion.1
  125.2 0.2 dynamic-slice_reduce_fusion
  125.4 0.6 copy.35
  126.0 0.8 copy.36
  126.8 1.1 reshape.70
  128.0 1.3 copy.32
  129.3 0.9 copy.33
  130.2 2.1 reshape.68
  132.3 870.0 %all-to-all-done.2 = bf16[16,896,2048]{2,1,0:T(8,128)(2,1)} async-done(((bf16[16,896,2048]{2,1,0:T(8,128)(2,1)}), bf16[16,896,2048]{2,1,0:T(8,128)(2,1)}, u32[]{:S(2)}, u32[]{:S(2)}) %all-to-all-start.2) | async-done | bytes 58720288 | tf_op jit(solution)/shard_map/all_to_all | solution.py:55
  1002.2 38.9 %fusion.6 = (bf16[16,896,1024]{2,1,0:T(8,128)(2,1)}, bf16[16,896,1024]{2,1,0:T(8,128)(2,1)}) fusion(bf16[16,896,2048]{2,1,0:T(8,128)(2,1)} %all-to-all-done.2), kind=kLoop, calls=%fused_computation.25 | loop fusion | bytes 117440512 | tf_op jit(solution)/shard_map/gather | solution.py:58
  1041.2 11.9 %gather_fusion = bf16[2,896,1024]{2,1,0:T(8,128)(2,1)} fusion(bf16[16,896,1024]{2,1,0:T(8,128)(2,1)} %get-tuple-element.3, s32[1024]{0:T(1024)S(1)} %pad_clamp_fusion), kind=kCustom, calls=%fused_computation | custom fusion | bytes 7340040 | tf_op jit(solution)/shard_map/gather | solution.py:58
  1053.1 12.0 %gather_fusion.1 = bf16[2,896,1024]{2,1,0:T(8,128)(2,1)} fusion(bf16[16,896,1024]{2,1,0:T(8,128)(2,1)} %get-tuple-element.4, s32[1024]{0:T(1024)S(1)} %pad_clamp_fusion), kind=kCustom, calls=%fused_computation.1 | custom fusion | bytes 7340040 | tf_op jit(solution)/shard_map/gather | solution.py:58
  1065.0 8.9 fusion
  (3 shorter events, 0.0 us)
Async XLA Ops:
  7.2 40.7 %copy-start = (s32[16,2]{0,1:T(2,128)S(1)}, s32[16,2]{0,1:T(2,128)}, u32[]{:S(2)}) copy-start(s32[16,2]{0,1:T(2,128)} %param.17) | copy-start | bytes 388
  7.2 30.4 %all-gather.7.cloned.1.call-start = ((), (), s32[]{:S(2)}) async-start(), calls=%async_computation.4 | async-start | bytes 1179648 | tf_op jit(solution)/shard_map/all_gather | solution.py:34
  11.7 55.9 %all-gather.5.cloned.1.call-start = ((), (), s32[]{:S(2)}) async-start(), calls=%async_computation.3 | async-start | bytes 3538944 | tf_op jit(solution)/shard_map/all_gather | solution.py:33
  40.9 32.6 %all-to-all-start.1 = ((bf16[32,16,1024]{2,0,1:T(8,128)(2,1)}), bf16[32,16,1024]{2,0,1:T(8,128)(2,1)S(1)}, u32[]{:S(2)}, u32[]{:S(2)}) async-start(bf16[32,16,1024]{2,0,1:T(8,128)(2,1)} %copy.34), calls=%async_computation.1 | async-start | bytes 2097152 | tf_op jit(solution)/shard_map/all_to_all | solution.py:38
  73.5 44.1 %all-to-all-start = ((bf16[96,16,768]{2,0,1:T(8,128)(2,1)}), bf16[96,16,768]{2,0,1:T(8,128)(2,1)S(1)}, u32[]{:S(2)}, u32[]{:S(2)}) async-start(bf16[96,16,768]{2,0,1:T(8,128)(2,1)} %copy.31), calls=%async_computation | async-start | bytes 4718592 | tf_op jit(solution)/shard_map/all_to_all | solution.py:37
  101.6 23.1 %copy-start.1 = (s32[16]{0:T(128)S(1)}, s32[16]{0:T(128)}, u32[]{:S(2)}) copy-start(s32[16]{0:T(128)} %param.16) | copy-start | bytes 196
  117.6 884.6 %all-to-all-start.2 = ((bf16[16,896,2048]{2,1,0:T(8,128)(2,1)}), bf16[16,896,2048]{2,1,0:T(8,128)(2,1)}, u32[]{:S(2)}, u32[]{:S(2)}) async-start(bf16[16,896,2048]{2,1,0:T(8,128)(2,1)} %broadcast_select_fusion), calls=%async_computation.2 | async-start | bytes 117440512 | tf_op jit(solution)/shard_map/all_to_all | solution.py:55
Sparse Core Ops, SparseCore 0:
  11.8 25.7 all-gather.6
  39.8 27.6 all-gather.4
where the time goes:
time: 1080 us
  waiting for transfers between devices  917 us (85%)
  local copies, waits for them, and re-layouts  80.7 us (7%)
  other arithmetic  45.9 us (4%)
  starting transfers between devices  21.1 us (2%)
  between operations  16.1 us (1%)
    all_to_all x1, waiting for transfers between devices, per_device(): lax.all_to_all(outgoing, 'tensor', split_axis=0, concat_axis=0, tiled=True)  870 us
    gather x3, local copies, waits for them, and re-layouts, per_device(): picked = received[own_stored]  62.8 us
  transfers between devices with their start and end apart: 5, of which 4 were waited for; matrix products, arithmetic and copies ran while one was open for 4% of the time, Pallas kernels for 0%

commit v1 on v0

v1 whole, which is shorter than its diff:
```python
import jax
import jax.numpy as jnp
from jax import lax
from jax.sharding import PartitionSpec as P


def publish(weight_part, state_part, rate):
    return (rate * state_part + (1.0 - rate) * weight_part.astype(jnp.float32)).astype(jnp.bfloat16)


def serve_columns(block, host_count):
    rows, width = block.shape
    split = block.reshape(rows, host_count, width // host_count).transpose(1, 0, 2)
    moved = lax.all_to_all(split, "tensor", split_axis=0, concat_axis=0, tiled=True)
    return lax.all_gather(moved.reshape(host_count * rows, width // host_count), "dp", axis=0, tiled=True)


def per_device(
    query_weight,
    query_state,
    latent_weight,
    latent_state,
    expert_weight,
    expert_state,
    decay,
    shard_expert,
    host_slots,
):
    host_count = lax.axis_size("tensor")
    query_serving = serve_columns(publish(query_weight, query_state, decay[0]), host_count)
    latent_serving = serve_columns(publish(latent_weight, latent_state, decay[1]), host_count)

    blended = publish(expert_weight[0], expert_state[0], decay[2])
    rows, width = blended.shape
    chunk = rows // host_count
    count = shard_expert.shape[0]
    ids = jnp.arange(count, dtype=jnp.int32)
    inverse = jnp.sum(jnp.where(shard_expert[None, :] == ids[:, None], ids[None, :], 0), axis=1)
    slot_clamped = jnp.maximum(host_slots, 0)
    stored = jnp.sum(
        jnp.where(slot_clamped[:, :, None] == ids[None, None, :], inverse[None, None, :], 0), axis=2
    )
    spread = lax.all_to_all(
        blended.reshape(host_count, chunk, width), "tensor", split_axis=0, concat_axis=0, tiled=True
    )
    outgoing = spread[stored.reshape(-1)].reshape(host_count, host_slots.shape[1], chunk, width)
    received = lax.all_to_all(outgoing, "tensor", split_axis=0, concat_axis=0, tiled=True)
    own_filled = lax.dynamic_index_in_dim(host_slots, lax.axis_index("tensor"), 0, keepdims=False) >= 0
    slots = received.transpose(1, 0, 2, 3).reshape(1, host_slots.shape[1], rows, width)
    expert_serving = jnp.where(own_filled[None, :, None, None], slots, jnp.zeros_like(slots))
    return (query_serving, latent_serving, expert_serving)


def solution(mesh):
    placed = (
        P(("dp", "tensor"), None),
        P(("dp", "tensor"), None),
        P(("dp", "tensor"), None),
        P(("dp", "tensor"), None),
        P("tensor", "dp", None),
        P("tensor", "dp", None),
        P(),
        P(),
        P(),
    )
    return jax.shard_map(
        per_device,
        mesh=mesh,
        in_specs=placed,
        out_specs=(P(None, "tensor"), P(None, "tensor"), P("tensor", None, "dp", None)),
        check_vma=False,
    )
```

time: 1080 us -> 229 us (0.21)
  waiting for transfers between devices: 917 us -> 155 us
  local copies, waits for them, and re-layouts: 80.7 us -> 16.9 us
  other arithmetic: 45.9 us -> 15.4 us
    all_to_all x1, waiting for transfers between devices: 870 us -> 46.9 us  [per_device(): lax.all_to_all(outgoing, 'tensor', split_axis=0, concat_axis=0, tiled=True)]
    gather x3 -> x1, local copies, waits for them, and re-layouts: 62.8 us -> 6.1 us  [per_device(): spread[stored.reshape(-1)]]
    all_to_all x2 -> x3, waiting for transfers between devices: 16 us -> 54.6 us  [the longest x1 51.3 us: per_device(): lax.all_to_all(blended.reshape(host_count, chunk, width), 'tensor', split...]
    select_n x3 -> x2, other arithmetic: 30 us -> 3.6 us  [the longest x1 3.59 us: per_device(): jnp.where(own_filled[None, :, None, None], slots, jnp.zeros_like(slots))]
    all_gather x2, waiting for transfers between devices: 31 us -> 53.9 us  [serve_columns(): lax.all_gather(moved.reshape(host_count * rows, width // host_count), 'dp...]
    convert_element_type x0 -> x3, other arithmetic: none -> 11.3 us  [publish(): (rate * state_part + (1.0 - rate) * weight_part.astype(jnp.float32)).asty...]
    all_to_all x6 -> x0, local copies, waits for them, and re-layouts: 11.2 us -> none  [the longest x3 7.27 us: per_device(): lax.all_to_all(query_rows, 'tensor', split_axis=1, concat_axis=0, tiled=T...]
  transfers between devices with their start and end apart: 5 -> 6, of which waited for: 4 -> 5; matrix products, arithmetic and copies ran while one was open for 4% -> 8% of each run, Pallas kernels for 0% -> 0%
where the time goes in v1:
time: 229 us; the launch traced here: 228 us
  waiting for transfers between devices  155 us (68%)
  starting transfers between devices  24.5 us (11%)
  local copies, waits for them, and re-layouts  16.9 us (7%)
  between operations  16.1 us (7%)
  other arithmetic  15.4 us (7%)
    all_gather x2, waiting for transfers between devices, serve_columns(): lax.all_gather(moved.reshape(host_count * rows, width // host_count), 'dp...  53.9 us
    all_to_all x1, waiting for transfers between devices, per_device(): lax.all_to_all(blended.reshape(host_count, chunk, width), 'tensor', split...  51.3 us
    all_to_all x1, waiting for transfers between devices, per_device(): lax.all_to_all(outgoing, 'tensor', split_axis=0, concat_axis=0, tiled=True)  46.9 us
    all_to_all x2, starting transfers between devices, serve_columns(): lax.all_to_all(split, 'tensor', split_axis=0, concat_axis=0, tiled=True)  12.3 us
    convert_element_type x3, other arithmetic, publish(): (rate * state_part + (1.0 - rate) * weight_part.astype(jnp.float32)).asty...  11.3 us
    all_to_all x1, starting transfers between devices, per_device(): lax.all_to_all(blended.reshape(host_count, chunk, width), 'tensor', split...  7.41 us
    gather x1, local copies, waits for them, and re-layouts, per_device(): spread[stored.reshape(-1)]  6.1 us
    all_to_all x1, starting transfers between devices, per_device(): lax.all_to_all(outgoing, 'tensor', split_axis=0, concat_axis=0, tiled=True)  4.7 us
  transfers between devices with their start and end apart: 6, of which 5 were waited for; matrix products, arithmetic and copies ran while one was open for 8% of the time, Pallas kernels for 0%

profile of v1, /device:TPU:0, one launch (start us, length us, event | category | flops | bytes accessed | tf_op | source)
XLA Modules:
  0.0 228.2 jit_solution(7825675435248695792)
XLA Ops:
  7.2 1.4 fusion.1
  9.2 2.4 %add_convert_fusion.2 = bf16[4,16384]{1,0:T(4,128)(2,1)} fusion(bf16[4,16384]{1,0:T(4,128)(2,1)} %param.11, f32[4,16384]{1,0:T(4,128)} %param.12, f32[]{:T(128)S(6)} %sub.10, f32[]{:T(128)} %bitcast.2), kind=kLoop, calls=%fused_computation.5 | loop fusion | flops 327680 | bytes 524296 | tf_op jit(solution)/shard_map/convert_element_type | solution.py:8
  11.6 8.0 %all-to-all-start.1 = ((bf16[16,4,1024]{2,1,0:T(4,128)(2,1)}), bf16[16,4,1024]{2,1,0:T(4,128)(2,1)S(1)}, u32[]{:S(2)}, u32[]{:S(2)}) async-start(bf16[16,4,1024]{2,1,0:T(4,128)(2,1)} %bitcast.4), calls=%async_computation.1 | async-start | bytes 262144 | tf_op jit(solution)/shard_map/all_to_all | solution.py:14
  20.2 8.2 %add_convert_fusion = bf16[1,896,2048]{2,1,0:T(8,128)(2,1)} fusion(bf16[1,896,2048]{2,1,0:T(8,128)(2,1)} %param.13, f32[1,896,2048]{2,1,0:T(8,128)} %param.14, f32[]{:T(128)S(6)} %sub.11, f32[]{:T(128)} %bitcast.5), kind=kLoop, calls=%fused_computation.1 | loop fusion | flops 9175040 | bytes 14680072 | tf_op jit(solution)/shard_map/convert_element_type | solution.py:8
  28.4 0.0 copy-start.5
  28.4 0.0 copy-start.4
  28.4 0.0 copy-start.2
  28.4 0.0 copy-start.3
  28.5 0.0 all-to-all-done.1
  28.5 7.4 %all-to-all-start.2 = ((bf16[16,56,2048]{2,1,0:T(8,128)(2,1)}), bf16[16,56,2048]{2,1,0:T(8,128)(2,1)}, u32[]{:S(2)}, u32[]{:S(2)}) async-start(bf16[16,56,2048]{2,1,0:T(8,128)(2,1)} %bitcast.20), calls=%async_computation.2 | async-start | bytes 7340032 | tf_op jit(solution)/shard_map/all_to_all | solution.py:43
  35.9 0.0 copy-done.5
  35.9 0.1 select_reduce_fusion.1
  36.0 0.0 copy-done.4
  36.0 0.2 select_reduce_fusion
  36.2 0.1 copy.24
  36.3 0.1 reshape.93
  36.9 0.0 copy-done.2
  37.0 0.0 copy-done.3
  37.0 0.7 add_convert_fusion.1
  37.6 0.1 copy.26
  37.7 0.8 copy.28
  38.6 51.3 %all-to-all-done.2 = bf16[16,56,2048]{2,1,0:T(8,128)(2,1)} async-done(((bf16[16,56,2048]{2,1,0:T(8,128)(2,1)}), bf16[16,56,2048]{2,1,0:T(8,128)(2,1)}, u32[]{:S(2)}, u32[]{:S(2)}) %all-to-all-start.2) | async-done | bytes 3670048 | tf_op jit(solution)/shard_map/all_to_all | solution.py:43
  89.9 4.3 %all-to-all-start = ((bf16[16,12,768]{2,1,0:T(8,128)(2,1)}), bf16[16,12,768]{2,1,0:T(8,128)(2,1)S(1)}, u32[]{:S(2)}, u32[]{:S(2)}) async-start(bf16[16,12,768]{2,1,0:T(8,128)(2,1)} %bitcast.17), calls=%async_computation | async-start | bytes 786432 | tf_op jit(solution)/shard_map/all_to_all | solution.py:14
  94.2 6.1 %gather_fusion = bf16[32,56,2048]{2,1,0:T(8,128)(2,1)} fusion(bf16[16,56,2048]{2,1,0:T(8,128)(2,1)} %all-to-all-done.2, s32[1024]{0:T(1024)S(1)} %pad_clamp_fusion), kind=kCustom, calls=%fused_computation | custom fusion | bytes 14680192 | tf_op jit(solution)/shard_map/gather | solution.py:46
  100.3 3.3 %all-to-all-done = bf16[16,12,768]{2,1,0:T(8,128)(2,1)S(1)} async-done(((bf16[16,12,768]{2,1,0:T(8,128)(2,1)}), bf16[16,12,768]{2,1,0:T(8,128)(2,1)S(1)}, u32[]{:S(2)}, u32[]{:S(2)}) %all-to-all-start) | async-done | bytes 294944 | tf_op jit(solution)/shard_map/all_to_all | solution.py:14
  103.6 4.7 %all-to-all-start.3 = ((bf16[16,2,56,2048]{3,2,1,0:T(8,128)(2,1)}), bf16[16,2,56,2048]{3,2,1,0:T(8,128)(2,1)}, u32[]{:S(2)}, u32[]{:S(2)}) async-start(bf16[16,2,56,2048]{3,2,1,0:T(8,128)(2,1)} %bitcast.18), calls=%async_computation.3 | async-start | bytes 14680064 | tf_op jit(solution)/shard_map/all_to_all | solution.py:47
  108.3 0.0 all-gather.5.cloned.1.call-start
  108.4 0.7 reshape.92
  109.1 0.0 all-gather.5.cloned.1.call-update
  109.1 0.0 all-gather.3.cloned.1.call-start
  109.1 0.8 reshape.90
  109.9 0.0 all-gather.3.cloned.1.call-update
  109.9 0.2 compare_reduce_fusion
  110.1 26.2 %all-gather.5.cloned.1.call-done = bf16[512,1024]{1,0:T(8,128)(2,1)} async-done(((bf16[64,1024]{1,0:T(8,128)(2,1)}), bf16[512,1024]{1,0:T(8,128)(2,1)}) %all-gather.5.cloned.1.call-update) | async-done | bytes 1048592 | tf_op jit(solution)/shard_map/all_gather | solution.py:15
  136.3 27.7 %all-gather.3.cloned.1.call-done = bf16[1536,768]{1,0:T(8,128)(2,1)} async-done(((bf16[192,768]{1,0:T(8,128)(2,1)}), bf16[1536,768]{1,0:T(8,128)(2,1)}) %all-gather.3.cloned.1.call-update) | async-done | bytes 2359312 | tf_op jit(solution)/shard_map/all_gather | solution.py:15
  164.0 46.9 %all-to-all-done.3 = bf16[16,2,56,2048]{3,2,1,0:T(8,128)(2,1)} async-done(((bf16[16,2,56,2048]{3,2,1,0:T(8,128)(2,1)}), bf16[16,2,56,2048]{3,2,1,0:T(8,128)(2,1)}, u32[]{:S(2)}, u32[]{:S(2)}) %all-to-all-start.3) | async-done | bytes 7340064 | tf_op jit(solution)/shard_map/all_to_all | solution.py:47
  210.9 4.5 %copy.25 = bf16[2,16,56,2048]{3,2,1,0:T(8,128)(2,1)S(1)} copy(bf16[2,16,56,2048]{3,2,0,1:T(8,128)(2,1)} %bitcast.9) | data formatting | bytes 14680064 | tf_op jit(solution)/shard_map/transpose | solution.py:49
  215.4 0.0 copy-start
  215.4 0.0 copy-start.1
  215.4 3.6 %broadcast_select_fusion = bf16[1,2,896,2048]{3,2,1,0:T(8,128)(2,1)} fusion(bf16[1,2,896,2048]{3,2,1,0:T(8,128)(2,1)S(1)} %bitcast.19, pred[2]{0:T(512)(128)(4,1)S(1)} %compare_reduce_fusion), kind=kLoop, calls=%fused_computation.2 | loop fusion | flops 3670016 | bytes 14680066 | tf_op jit(solution)/shard_map/jit(_where)/select_n | solution.py:50
  219.0 0.0 copy-done
  219.0 1.4 copy.31
  220.4 0.0 copy-done.1
  220.4 1.0 copy.32
  (4 shorter events, 0.0 us)
Async XLA Ops:
  11.6 16.9 %all-to-all-start.1 = ((bf16[16,4,1024]{2,1,0:T(4,128)(2,1)}), bf16[16,4,1024]{2,1,0:T(4,128)(2,1)S(1)}, u32[]{:S(2)}, u32[]{:S(2)}) async-start(bf16[16,4,1024]{2,1,0:T(4,128)(2,1)} %bitcast.4), calls=%async_computation.1 | async-start | bytes 262144 | tf_op jit(solution)/shard_map/all_to_all | solution.py:14
  28.4 7.4 %copy-start.5 = (s32[16]{0:T(128)S(1)}, s32[16]{0:T(128)}, u32[]{:S(2)}) copy-start(s32[16]{0:T(128)} %param.16) | copy-start | bytes 196
  28.4 7.6 %copy-start.4 = (s32[16,2]{0,1:T(2,128)S(1)}, s32[16,2]{0,1:T(2,128)}, u32[]{:S(2)}) copy-start(s32[16,2]{0,1:T(2,128)} %param.17) | copy-start | bytes 388
  28.4 8.5 %copy-start.2 = (f32[12,12288]{1,0:T(8,128)S(1)}, f32[12,12288]{1,0:T(8,128)}, u32[]{:S(2)}) copy-start(f32[12,12288]{1,0:T(8,128)} %param.10) | copy-start | bytes 1769476
  28.4 8.5 %copy-start.3 = (bf16[12,12288]{1,0:T(8,128)(2,1)S(1)}, bf16[12,12288]{1,0:T(8,128)(2,1)}, u32[]{:S(2)}) copy-start(bf16[12,12288]{1,0:T(8,128)(2,1)} %param.9) | copy-start | bytes 884740
  28.5 61.4 %all-to-all-start.2 = ((bf16[16,56,2048]{2,1,0:T(8,128)(2,1)}), bf16[16,56,2048]{2,1,0:T(8,128)(2,1)}, u32[]{:S(2)}, u32[]{:S(2)}) async-start(bf16[16,56,2048]{2,1,0:T(8,128)(2,1)} %bitcast.20), calls=%async_computation.2 | async-start | bytes 7340032 | tf_op jit(solution)/shard_map/all_to_all | solution.py:43
  89.9 13.7 %all-to-all-start = ((bf16[16,12,768]{2,1,0:T(8,128)(2,1)}), bf16[16,12,768]{2,1,0:T(8,128)(2,1)S(1)}, u32[]{:S(2)}, u32[]{:S(2)}) async-start(bf16[16,12,768]{2,1,0:T(8,128)(2,1)} %bitcast.17), calls=%async_computation | async-start | bytes 786432 | tf_op jit(solution)/shard_map/all_to_all | solution.py:14
  103.6 107.3 %all-to-all-start.3 = ((bf16[16,2,56,2048]{3,2,1,0:T(8,128)(2,1)}), bf16[16,2,56,2048]{3,2,1,0:T(8,128)(2,1)}, u32[]{:S(2)}, u32[]{:S(2)}) async-start(bf16[16,2,56,2048]{3,2,1,0:T(8,128)(2,1)} %bitcast.18), calls=%async_computation.3 | async-start | bytes 14680064 | tf_op jit(solution)/shard_map/all_to_all | solution.py:47
  108.3 28.0 %all-gather.5.cloned.1.call-start = ((), (), s32[]{:S(2)}) async-start(), calls=%async_computation.5 | async-start | bytes 1179648 | tf_op jit(solution)/shard_map/all_gather | solution.py:15
  109.1 55.0 %all-gather.3.cloned.1.call-start = ((), (), s32[]{:S(2)}) async-start(), calls=%async_computation.4 | async-start | bytes 2654208 | tf_op jit(solution)/shard_map/all_gather | solution.py:15
  215.4 3.6 %copy-start = (bf16[1536,768]{1,0:T(8,128)(2,1)S(1)}, bf16[1536,768]{1,0:T(8,128)(2,1)}, u32[]{:S(2)}) copy-start(bf16[1536,768]{1,0:T(8,128)(2,1)} %all-gather.3.cloned.1.call-done) | copy-start | bytes 7077892
  215.4 5.0 %copy-start.1 = (bf16[512,1024]{1,0:T(8,128)(2,1)S(1)}, bf16[512,1024]{1,0:T(8,128)(2,1)}, u32[]{:S(2)}) copy-start(bf16[512,1024]{1,0:T(8,128)(2,1)} %all-gather.5.cloned.1.call-done) | copy-start | bytes 3145732
Sparse Core Ops, SparseCore 0:
  111.4 24.8 all-gather.4
  138.6 25.4 all-gather.2

commit v2 on v1

--- a/solution.py
+++ b/solution.py
@@ -1,7 +1,13 @@
 import jax
 import jax.numpy as jnp
 from jax import lax
+from jax.experimental import pallas as pl
+from jax.experimental.pallas import tpu as pltpu
 from jax.sharding import PartitionSpec as P
+
+MESH = pl.DeviceIdType.MESH
+SIDE = 4
+SPLITS = 4
 
 
 def publish(weight_part, state_part, rate):
@@ -13,6 +19,208 @@
     split = block.reshape(rows, host_count, width // host_count).transpose(1, 0, 2)
     moved = lax.all_to_all(split, "tensor", split_axis=0, concat_axis=0, tiled=True)
     return lax.all_gather(moved.reshape(host_count * rows, width // host_count), "dp", axis=0, tiled=True)
+
+
+def expert_kernel(stored_ref, decay_ref, weight_ref, state_ref, out_ref, *scratch):
+    rows, width = weight_ref.shape
+    half, cols = rows // 2, width // SPLITS
+    part = half // SIDE
+    pieces = [(h, k) for k in range(SPLITS) for h in range(2)]
+    count = len(pieces)
+    wbuf, sbuf, own, staged = scratch[:4]
+    gathered = scratch[4 : 4 + count]
+    (load_sem, local_sem, spread_send, spread_recv, ring_send, ring_recv, relay_send, relay_recv,
+     deliver_send, deliver_recv, keep_sem) = scratch[4 + count :]
+
+    position = lax.axis_index("tensor")
+    here = (position % SIDE, position // SIDE)
+
+    def device(h, u, v):
+        return v * SIDE + u if h == 0 else u * SIDE + v
+
+    def coords(h):
+        return (here[0], here[1]) if h == 0 else (here[1], here[0])
+
+    def shifted(a, d):
+        return (a + d) % SIDE
+
+    loads = []
+    for i, (h, k) in enumerate(pieces):
+        window = (pl.ds(half * h, half), pl.ds(cols * k, cols))
+        pair = (
+            pltpu.make_async_copy(weight_ref.at[window], wbuf.at[i], load_sem.at[i, 0]),
+            pltpu.make_async_copy(state_ref.at[window], sbuf.at[i], load_sem.at[i, 1]),
+        )
+        for copy in pair:
+            copy.start()
+        loads.append(pair)
+
+    barrier = pltpu.get_barrier_semaphore()
+    for h in range(2):
+        u, v = coords(h)
+        for d in range(1, SIDE):
+            pl.semaphore_signal(
+                barrier, inc=1, device_id={"tensor": device(h, shifted(u, d), v)}, device_id_type=MESH
+            )
+
+    rate = decay_ref[2]
+    rest = 1.0 - rate
+    step = 16
+
+    def blend(i):
+        for copy in loads[i]:
+            copy.wait()
+
+        def body(r, carry):
+            at = pl.ds(pl.multiple_of(r * step, step), step)
+            own[i, at, :] = (rate * sbuf[i, at, :] + rest * wbuf[i, at, :].astype(jnp.float32)).astype(
+                jnp.bfloat16
+            )
+            return carry
+
+        lax.fori_loop(0, half // step, body, 0)
+
+    def send(src, dst, send_sem, recv_sem, target):
+        copy = pltpu.make_async_remote_copy(
+            src_ref=src, dst_ref=dst, send_sem=send_sem, recv_sem=recv_sem,
+            device_id={"tensor": target}, device_id_type=MESH,
+        )
+        copy.start()
+        return copy
+
+    def row_part(u):
+        return pl.ds(pl.multiple_of(u * part, 16), part)
+
+    def spread(i):
+        h, _ = pieces[i]
+        u, v = coords(h)
+        mine = v * SIDE + u
+        copies = [
+            send(own.at[i, row_part(shifted(u, d))], gathered[i].at[mine], spread_send.at[i, d - 1],
+                 spread_recv.at[i, d - 1], device(h, shifted(u, d), v))
+            for d in (1, 3, 2)
+        ]
+        local = pltpu.make_async_copy(own.at[i, row_part(u)], gathered[i].at[mine], local_sem.at[i])
+        local.start()
+        return copies, local
+
+    sent = []
+    spreads = []
+    blend(0)
+    pl.semaphore_wait(barrier, 2 * (SIDE - 1))
+    for i in range(1, count):
+        blend(i)
+        spreads.append(spread(i - 1))
+    spreads.append(spread(count - 1))
+
+    rings = []
+    for i, (h, k) in enumerate(pieces):
+        u, v = coords(h)
+        copies, local = spreads[i]
+        for copy in copies:
+            copy.wait_recv()
+        local.wait()
+        sent += copies
+        group = gathered[i].at[pl.ds(v * SIDE, SIDE)]
+        rings.append([
+            send(group, group, ring_send.at[i, n], ring_recv.at[i, n], device(h, u, shifted(v, d)))
+            for n, d in enumerate((1, 3))
+        ])
+
+    relays = []
+    for i, (h, k) in enumerate(pieces):
+        u, v = coords(h)
+        for copy in rings[i]:
+            copy.wait_recv()
+        sent += rings[i]
+        ahead = gathered[i].at[pl.ds(shifted(v, 3) * SIDE, SIDE // 2)]
+        back = gathered[i].at[pl.ds(shifted(v, 1) * SIDE + SIDE // 2, SIDE // 2)]
+        relays.append([
+            send(ahead, ahead, relay_send.at[i, 0], relay_recv.at[i, 0], device(h, u, shifted(v, 1))),
+            send(back, back, relay_send.at[i, 1], relay_recv.at[i, 1], device(h, u, shifted(v, 3))),
+        ])
+
+    delivered = []
+    kept = []
+    for k in range(SPLITS):
+        for h in range(2):
+            i = 2 * k + h
+            u, v = coords(h)
+            for copy in relays[i]:
+                copy.wait_recv()
+            sent += relays[i]
+            for d in (1, 3, 2, 0):
+                to = shifted(u, d)
+                for s in range(2):
+                    staged[i, d, s] = gathered[i][stored_ref[h, device(h, to, v), s]]
+        for h in range(2):
+            i = 2 * k + h
+            u, v = coords(h)
+            window = out_ref.at[
+                :, pl.ds(pl.multiple_of(half * h + u * part, 16), part), pl.ds(cols * k, cols)
+            ]
+            delivered += [
+                send(staged.at[i, d], window, deliver_send.at[i, d - 1], deliver_recv.at[i, d - 1],
+                     device(h, shifted(u, d), v))
+                for d in (1, 3, 2)
+            ]
+            keep = pltpu.make_async_copy(staged.at[i, 0], window, keep_sem.at[i])
+            keep.start()
+            kept.append(keep)
+
+    for copy in kept:
+        copy.wait()
+    for copy in delivered:
+        copy.wait_recv()
+    for copy in sent + delivered:
+        copy.wait_send()
+
+
+def exchange(stored, decay, weight, state):
+    rows, width = weight.shape
+    count = 2 * SPLITS
+    half, cols = rows // 2, width // SPLITS
+    part = half // SIDE
+    hosts, slots = stored.shape
+    tables = jnp.stack([stored, stored % SIDE * SIDE + stored // SIDE])
+    dma = pltpu.SemaphoreType.DMA
+    hop = SIDE - 1
+    return pl.pallas_call(
+        expert_kernel,
+        name="expert_exchange",
+        out_shape=jax.ShapeDtypeStruct((slots, rows, width), jnp.bfloat16),
+        in_specs=[
+            pl.BlockSpec(memory_space=pltpu.SMEM),
+            pl.BlockSpec(memory_space=pltpu.SMEM),
+            pl.BlockSpec(memory_space=pl.ANY),
+            pl.BlockSpec(memory_space=pl.ANY),
+        ],
+        out_specs=pl.BlockSpec(memory_space=pl.ANY),
+        scratch_shapes=[
+            pltpu.VMEM((count, half, cols), jnp.bfloat16),
+            pltpu.VMEM((count, half, cols), jnp.float32),
+            pltpu.VMEM((count, half, cols), jnp.bfloat16),
+            pltpu.VMEM((count, SIDE, slots, part, cols), jnp.bfloat16),
+        ]
+        + [pltpu.VMEM((hosts, part, cols), jnp.bfloat16)] * count
+        + [
+            dma((count, 2)),
+            dma((count,)),
+            dma((count, hop)),
+            dma((count, hop)),
+            dma((count, 2)),
+            dma((count, 2)),
+            dma((count, 2)),
+            dma((count, 2)),
+            dma((count, hop)),
+            dma((count, hop)),
+            dma((count,)),
+        ],
+        compiler_params=pltpu.CompilerParams(
+            collective_id=0, has_side_effects=True, vmem_limit_bytes=48 * 2**20
+        ),
+        cost_estimate=pl.CostEstimate(flops=0, bytes_accessed=400_000_000, transcendentals=0),
+    )(tables, decay, weight, state)
 
 
 def per_device(
@@ -30,9 +238,6 @@
     query_serving = serve_columns(publish(query_weight, query_state, decay[0]), host_count)
     latent_serving = serve_columns(publish(latent_weight, latent_state, decay[1]), host_count)
 
-    blended = publish(expert_weight[0], expert_state[0], decay[2])
-    rows, width = blended.shape
-    chunk = rows // host_count
     count = shard_expert.shape[0]
     ids = jnp.arange(count, dtype=jnp.int32)
     inverse = jnp.sum(jnp.where(shard_expert[None, :] == ids[:, None], ids[None, :], 0), axis=1)
@@ -40,13 +245,8 @@
     stored = jnp.sum(
         jnp.where(slot_clamped[:, :, None] == ids[None, None, :], inverse[None, None, :], 0), axis=2
     )
-    spread = lax.all_to_all(
-        blended.reshape(host_count, chunk, width), "tensor", split_axis=0, concat_axis=0, tiled=True
-    )
-    outgoing = spread[stored.reshape(-1)].reshape(host_count, host_slots.shape[1], chunk, width)
-    received = lax.all_to_all(outgoing, "tensor", split_axis=0, concat_axis=0, tiled=True)
+    slots = exchange(stored, decay, expert_weight[0], expert_state[0])[None]
     own_filled = lax.dynamic_index_in_dim(host_slots, lax.axis_index("tensor"), 0, keepdims=False) >= 0
-    slots = received.transpose(1, 0, 2, 3).reshape(1, host_slots.shape[1], rows, width)
     expert_serving = jnp.where(own_filled[None, :, None, None], slots, jnp.zeros_like(slots))
     return (query_serving, latent_serving, expert_serving)
 

time: 229 us -> 192 us (0.84)
  waiting for transfers between devices: 155 us -> 7.33 us
  Pallas kernels: 0 us -> 124 us
  starting transfers between devices: 24.5 us -> 8.07 us
  blocking collectives: 0 us -> 12.5 us
  local copies, waits for them, and re-layouts: 16.9 us -> 11.2 us
  other arithmetic: 15.4 us -> 13 us
    pallas_call x0 -> x1, Pallas kernels: none -> 124 us  [exchange(): pl.pallas_call(expert_kernel, name='expert_exchange', out_shape=jax.Shape...]
    all_to_all x2 -> x0, waiting for transfers between devices: 98.2 us -> none  [the longest x1 51.3 us: per_device(): lax.all_to_all(blended.reshape(host_count, chunk, width), 'tensor', split...]
    all_gather x2, waiting for transfers between devices: 53.9 us -> 0.01 us  [serve_columns(): lax.all_gather(moved.reshape(host_count * rows, width // host_count), 'dp...]
    all_to_all x0 -> x1, blocking collectives: none -> 12.5 us  [serve_columns(): lax.all_to_all(split, 'tensor', split_axis=0, concat_axis=0, tiled=True)]
    all_to_all x2 -> x0, starting transfers between devices: 12.1 us -> none  [the longest x1 7.41 us: per_device(): lax.all_to_all(blended.reshape(host_count, chunk, width), 'tensor', split...]
    convert_element_type x3 -> x2, other arithmetic: 11.3 us -> 4.43 us  [publish(): (rate * state_part + (1.0 - rate) * weight_part.astype(jnp.float32)).asty...]
    gather x1 -> x0, local copies, waits for them, and re-layouts: 6.1 us -> none  [per_device(): spread[stored.reshape(-1)]]
    unnamed x15 -> x9, local copies, waits for them, and re-layouts: 2.47 us -> 8.26 us
  transfers between devices with their start and end apart: 6 -> 3, of which waited for: 5 -> 1; matrix products, arithmetic and copies ran while one was open for 8% -> 6% of each run, Pallas kernels for 0% -> 65%
where the time goes in v2:
time: 192 us; the launch traced here: 191 us
  Pallas kernels  124 us (65%)
  between operations  15.4 us (8%)
  other arithmetic  13 us (7%)
  blocking collectives  12.5 us (7%)
  local copies, waits for them, and re-layouts  11.2 us (6%)
  starting transfers between devices  8.07 us (4%)
  waiting for transfers between devices  7.33 us (4%)
    pallas_call x1, Pallas kernels, exchange(): pl.pallas_call(expert_kernel, name='expert_exchange', out_shape=jax.Shape...  124 us
    all_to_all x1, blocking collectives, serve_columns(): lax.all_to_all(split, 'tensor', split_axis=0, concat_axis=0, tiled=True)  12.5 us
    unnamed x9, local copies, waits for them, and re-layouts  8.26 us
    all_to_all x1, starting transfers between devices, serve_columns(): lax.all_to_all(split, 'tensor', split_axis=0, concat_axis=0, tiled=True)  7.99 us
    all_to_all x1, waiting for transfers between devices, serve_columns(): lax.all_to_all(split, 'tensor', split_axis=0, concat_axis=0, tiled=True)  7.29 us
    select_n x1, other arithmetic, per_device(): jnp.where(own_filled[None, :, None, None], slots, jnp.zeros_like(slots))  6.68 us
    convert_element_type x2, other arithmetic, publish(): (rate * state_part + (1.0 - rate) * weight_part.astype(jnp.float32)).asty...  4.43 us
  transfers between devices with their start and end apart: 3, of which 1 were waited for; matrix products, arithmetic and copies ran while one was open for 6% of the time, Pallas kernels for 65%

profile of v2, /device:TPU:0, one launch (start us, length us, event | category | flops | bytes accessed | tf_op | source)
XLA Modules:
  0.0 191.1 jit_solution(7651473561159265917)
XLA Ops:
  7.2 1.3 fusion.2
  9.1 2.4 %add_convert_fusion.1 = bf16[4,16384]{1,0:T(4,128)(2,1)} fusion(bf16[4,16384]{1,0:T(4,128)(2,1)} %param.11, f32[4,16384]{1,0:T(4,128)} %param.12, f32[]{:T(128)S(6)} %sub.13, f32[]{:T(128)} %bitcast.2), kind=kLoop, calls=%fused_computation.3 | loop fusion | flops 327680 | bytes 524296 | tf_op jit(solution)/shard_map/convert_element_type | solution.py:14
  11.5 8.0 %all-to-all-start.1 = ((bf16[16,4,1024]{2,1,0:T(4,128)(2,1)}), bf16[16,4,1024]{2,1,0:T(4,128)(2,1)S(1)}, u32[]{:S(2)}, u32[]{:S(2)}) async-start(bf16[16,4,1024]{2,1,0:T(4,128)(2,1)} %bitcast.4), calls=%async_computation.1 | async-start | bytes 262144 | tf_op jit(solution)/shard_map/all_to_all | solution.py:20
  19.5 0.0 all-gather.5.cloned.1.call-start
  20.2 7.3 %all-to-all-done.1 = bf16[16,4,1024]{2,1,0:T(4,128)(2,1)S(1)} async-done(((bf16[16,4,1024]{2,1,0:T(4,128)(2,1)}), bf16[16,4,1024]{2,1,0:T(4,128)(2,1)S(1)}, u32[]{:S(2)}, u32[]{:S(2)}) %all-to-all-start.1) | async-done | bytes 131104 | tf_op jit(solution)/shard_map/all_to_all | solution.py:20
  27.5 0.7 reshape.108
  28.2 0.0 all-gather.5.cloned.1.call-update
  28.2 0.0 all-gather.3.cloned.1.call-start
  28.3 2.0 %add_convert_fusion = bf16[12,12288]{1,0:T(8,128)(2,1)S(1)} fusion(bf16[12,12288]{1,0:T(8,128)(2,1)} %param.9, f32[12,12288]{1,0:T(8,128)} %param.10, f32[]{:T(128)S(6)} %sub.12, f32[]{:T(128)} %bitcast), kind=kLoop, calls=%fused_computation.1 | loop fusion | flops 737280 | bytes 1179656 | tf_op jit(solution)/shard_map/convert_element_type | solution.py:14
  30.3 0.1 copy.35
  30.4 0.1 copy.37
  30.5 12.5 %all_to_all.10 = bf16[16,12,768]{2,1,0:T(8,128)(2,1)S(1)} all-to-all(bf16[16,12,768]{2,1,0:T(8,128)(2,1)S(1)} %bitcast.20), channel_id=1, replica_groups=mesh['dp'=8,'tensor'=16] {'tensor'}, dimensions={0} | all-to-all | bytes 589824 | tf_op jit(solution)/shard_map/all_to_all | solution.py:20
  43.0 0.8 reshape.106
  43.8 0.0 all-gather.3.cloned.1.call-update
  43.8 0.8 select_reduce_fusion.1
  44.6 0.7 broadcast_maximum_fusion
  45.3 0.2 select_reduce_fusion
  45.5 0.1 copy.34.stored_ref
  45.6 0.0 copy-start
  45.6 2.0 %copy-done = bf16[1,896,2048]{2,1,0:T(8,128)(2,1)S(1)} copy-done((bf16[1,896,2048]{2,1,0:T(8,128)(2,1)S(1)}, bf16[1,896,2048]{2,1,0:T(8,128)(2,1)}, u32[]{:S(2)}) %copy-start) | copy-done | bytes 3670040
  47.6 0.0 copy-start.1
  47.6 0.7 copy-done.1
  48.3 0.0 copy-start.2
  48.3 123.6 %expert_exchange.1 = bf16[2,896,2048]{2,1,0:T(8,128)(2,1)} custom-call(s32[2,16,2]{2,1,0:T(8,128)S(1)} %copy.34.stored_ref, f32[3]{0:T(128)S(1)} %copy-done.1, bf16[896,2048]{1,0:T(8,128)(2,1)S(1)} %bitcast.17, f32[896,2048]{1,0:T(8,128)} %bitcast.18), custom_call_target="tpu_custom_call" | custom-call | bytes 400000000 | tf_op jit(solution)/shard_map/expert_exchange/pallas_call | solution.py:188
  171.9 0.0 copy-done.2
  171.9 0.2 compare_reduce_fusion
  172.1 6.7 %select_bitcast_fusion = bf16[1,2,896,2048]{3,2,1,0:T(8,128)(2,1)} fusion(bf16[2,896,2048]{2,1,0:T(8,128)(2,1)} %expert_exchange.1, pred[2]{0:T(512)(128)(4,1)S(1)} %compare_reduce_fusion), kind=kLoop, calls=%fused_computation | loop fusion | flops 3670016 | bytes 14680066 | tf_op jit(solution)/shard_map/jit(_where)/select_n | solution.py:250
  178.8 0.0 all-gather.5.cloned.1.call-done
  178.8 0.0 all-gather.3.cloned.1.call-done
  178.8 3.2 %copy.40 = bf16[1536,768]{1,0:T(8,128)(2,1)} copy(bf16[1536,768]{1,0:T(8,128)(2,1)} %all-gather.3.cloned.1.call-done) | data formatting | bytes 4718592
  182.0 2.3 %copy.41 = bf16[512,1024]{1,0:T(8,128)(2,1)} copy(bf16[512,1024]{1,0:T(8,128)(2,1)} %all-gather.5.cloned.1.call-done) | data formatting | bytes 2097152
  (3 shorter events, 0.0 us)
Async XLA Ops:
  11.5 16.0 %all-to-all-start.1 = ((bf16[16,4,1024]{2,1,0:T(4,128)(2,1)}), bf16[16,4,1024]{2,1,0:T(4,128)(2,1)S(1)}, u32[]{:S(2)}, u32[]{:S(2)}) async-start(bf16[16,4,1024]{2,1,0:T(4,128)(2,1)} %bitcast.4), calls=%async_computation.1 | async-start | bytes 262144 | tf_op jit(solution)/shard_map/all_to_all | solution.py:20
  19.5 159.3 %all-gather.5.cloned.1.call-start = ((), (), s32[]{:S(2)}) async-start(), calls=%async_computation.3 | async-start | bytes 1179648 | tf_op jit(solution)/shard_map/all_gather | solution.py:21
  28.2 150.6 %all-gather.3.cloned.1.call-start = ((), (), s32[]{:S(2)}) async-start(), calls=%async_computation.2 | async-start | bytes 2654208 | tf_op jit(solution)/shard_map/all_gather | solution.py:21
  45.6 2.1 %copy-start = (bf16[1,896,2048]{2,1,0:T(8,128)(2,1)S(1)}, bf16[1,896,2048]{2,1,0:T(8,128)(2,1)}, u32[]{:S(2)}) copy-start(bf16[1,896,2048]{2,1,0:T(8,128)(2,1)} %param.13) | copy-start | bytes 11010052
  47.6 0.7 copy-start.1
  48.3 123.7 %copy-start.2 = (s32[16,2]{0,1:T(2,128)S(1)}, s32[16,2]{0,1:T(2,128)}, u32[]{:S(2)}) copy-start(s32[16,2]{0,1:T(2,128)} %param.17) | copy-start | bytes 388
Sparse Core Ops, SparseCore 0:
  28.4 21.0 all-gather.4
  51.7 25.5 all-gather.2

commit v3 on v1

v3 whole, which is shorter than its diff:
```python
import jax
import jax.numpy as jnp
from jax import lax
from jax.experimental import pallas as pl
from jax.experimental.pallas import tpu as pltpu
from jax.sharding import PartitionSpec as P

MESH = pl.DeviceIdType.MESH
SIDE = 4
HOSTS = SIDE * SIDE
SPLITS = 4
PIECES = tuple((h, k) for k in range(SPLITS) for h in range(2))
LOADED = 4
LANES = 128


def publish(weight, state, rate):
    return rate * state + (1.0 - rate) * weight.astype(jnp.float32)


def shifted(a, d):
    return (a + d) % SIDE


def send(src, dst, send_sem, recv_sem, target):
    copy = pltpu.make_async_remote_copy(
        src_ref=src, dst_ref=dst, send_sem=send_sem, recv_sem=recv_sem,
        device_id=target, device_id_type=MESH,
    )
    copy.start()
    return copy


def kernel(
    expert_table, slot_table, decay_table,
    query_weight, query_state, latent_weight, latent_state, expert_weight, expert_state,
    query_out, latent_out, expert_out,
    expert_of, slots_of, decay, table_sem, qw, qs, lw, ls, packed, crossed, heads, query_rows, latent_rows,
    wbuf, sbuf, own, staged, *rest,
):
    count = len(PIECES)
    gathered = rest[:count]
    (head_load, head_store, cross_send, cross_recv, cross_keep, column_send, column_recv, column_keep,
     dp_send, dp_recv, core_send, core_recv,
     load_sem, local_sem, spread_send, spread_recv, ring_send, ring_recv, relay_send, relay_recv,
     deliver_send, deliver_recv, keep_sem) = rest[count:]

    rows, width = expert_weight.shape
    half, cols = rows // 2, width // SPLITS
    part = half // SIDE
    qrows, qcols = query_weight.shape[0], query_weight.shape[1] // HOSTS
    lrows, lcols = latent_weight.shape[0], latent_weight.shape[1] // HOSTS
    qgroups, lgroups = qcols // LANES, lcols // LANES
    packed_rows = packed.shape[2]

    position = lax.axis_index("tensor")
    group = lax.axis_index("dp")
    x, z = position % SIDE, position // SIDE
    y, core = group // 2, group % 2

    def coords(h):
        return (x, z) if h == 0 else (z, x)

    def host(h, u, v):
        return v * SIDE + u if h == 0 else u * SIDE + v

    def line(h, d):
        u, v = coords(h)
        return {"tensor": host(h, shifted(u, d), v)}

    def along_y(d):
        return {"dp": shifted(y, d) * 2 + core}

    partner = {"dp": y * 2 + 1 - core}

    head_loads = [
        pltpu.make_async_copy(src, dst, head_load.at[n])
        for n, (src, dst) in enumerate(
            ((query_weight, qw), (query_state, qs), (latent_weight, lw), (latent_state, ls))
        )
    ]
    tables = [
        pltpu.make_async_copy(src, dst, table_sem.at[n])
        for n, (src, dst) in enumerate(
            ((expert_table, expert_of), (slot_table, slots_of), (decay_table, decay))
        )
    ]
    for copy in tables:
        copy.start()
    loads = []
    for i, (h, k) in enumerate(PIECES):
        window = (pl.ds(half * h, half), pl.ds(cols * k, cols))
        loads.append((
            pltpu.make_async_copy(expert_weight.at[window], wbuf.at[i % LOADED], load_sem.at[i, 0]),
            pltpu.make_async_copy(expert_state.at[window], sbuf.at[i % LOADED], load_sem.at[i, 1]),
        ))

    def start_load(i):
        for copy in loads[i]:
            copy.start()

    for i in range(2):
        start_load(i)
    for copy in head_loads:
        copy.start()
    for i in range(2, LOADED):
        start_load(i)

    barrier = pltpu.get_barrier_semaphore()
    greeted = [line(h, d) for h in range(2) for d in range(1, SIDE)] + [along_y(1), along_y(3), partner]
    for target in greeted:
        pl.semaphore_signal(barrier, inc=1, device_id=target, device_id_type=MESH)

    step = 16

    def blend(i):
        for copy in loads[i]:
            copy.wait()

        def body(r, carry):
            at = pl.ds(pl.multiple_of(r * step, step), step)
            own[i, at, :] = publish(wbuf[i % LOADED, at, :], sbuf[i % LOADED, at, :], decay[2]).astype(jnp.bfloat16)
            return carry

        lax.fori_loop(0, half // step, body, 0)
        if i + LOADED < count:
            start_load(i + LOADED)

    def row_part(u):
        return pl.ds(pl.multiple_of(u * part, 16), part)

    sent = []
    kept = []

    def spread(i):
        h, _ = PIECES[i]
        u, v = coords(h)
        mine = v * SIDE + u
        copies = [
            send(own.at[i, row_part(shifted(u, d))], gathered[i].at[mine], spread_send.at[i, d - 1],
                 spread_recv.at[i, d - 1], line(h, d))
            for d in (1, 3, 2)
        ]
        local = pltpu.make_async_copy(own.at[i, row_part(u)], gathered[i].at[mine], local_sem.at[i])
        local.start()
        return copies, local

    for copy in tables:
        copy.wait()
    spreads = []
    blend(0)
    blend(1)
    pl.semaphore_wait(barrier, len(greeted))
    spreads.append(spread(0))
    spreads.append(spread(1))

    for copy in head_loads:
        copy.wait()
    pad = jnp.zeros((packed_rows - qgroups * qrows - lgroups * lrows, LANES), jnp.float32)
    for t in range(HOSTS):
        q = publish(qw[:, t * qcols : (t + 1) * qcols], qs[:, t * qcols : (t + 1) * qcols], decay[0])
        l = publish(lw[:, t * lcols : (t + 1) * lcols], ls[:, t * lcols : (t + 1) * lcols], decay[1])
        strips = [q[:, g * LANES : (g + 1) * LANES] for g in range(qgroups)]
        strips += [l[:, g * LANES : (g + 1) * LANES] for g in range(lgroups)]
        packed[t // SIDE, t % SIDE] = jnp.concatenate(strips + [pad], axis=0).astype(jnp.bfloat16)

    blend(2)
    crossing = [
        send(packed.at[:, shifted(x, d)], crossed.at[x], cross_send.at[d - 1], cross_recv.at[d - 1], line(0, d))
        for d in (1, 3, 2)
    ]
    cross_local = pltpu.make_async_copy(packed.at[:, x], crossed.at[x], cross_keep)
    cross_local.start()

    for i in range(3, count):
        blend(i)
        spreads.append(spread(i - 1))
    spreads.append(spread(count - 1))

    for copy in crossing:
        copy.wait_recv()
    cross_local.wait()
    sent += crossing
    columns = [
        send(crossed.at[:, shifted(z, d)], heads.at[group, pl.ds(z * SIDE, SIDE)], column_send.at[d - 1],
             column_recv.at[d - 1], line(1, d))
        for d in (1, 3, 2)
    ]
    column_local = pltpu.make_async_copy(
        crossed.at[:, z], heads.at[group, pl.ds(z * SIDE, SIDE)], column_keep
    )
    column_local.start()

    rings = []
    for i, (h, k) in enumerate(PIECES):
        u, v = coords(h)
        copies, local = spreads[i]
        for copy in copies:
            copy.wait_recv()
        local.wait()
        sent += copies
        line_blocks = gathered[i].at[pl.ds(v * SIDE, SIDE)]
        rings.append([
            send(line_blocks, line_blocks, ring_send.at[i, n], ring_recv.at[i, n], line(1 - h, d))
            for n, d in enumerate((1, 3))
        ])

    for copy in columns:
        copy.wait_recv()
    column_local.wait()
    sent += columns
    mine = heads.at[group]
    turns = [send(mine, mine, dp_send.at[n], dp_recv.at[n], along_y(d)) for n, d in enumerate((1, 3))]
    swaps = [send(mine, mine, core_send.at[0], core_recv.at[0], partner)]

    relays = []
    for i, (h, k) in enumerate(PIECES):
        u, v = coords(h)
        for copy in rings[i]:
            copy.wait_recv()
        sent += rings[i]
        ahead = gathered[i].at[pl.ds(shifted(v, 3) * SIDE, SIDE // 2)]
        back = gathered[i].at[pl.ds(shifted(v, 1) * SIDE + SIDE // 2, SIDE // 2)]
        relays.append([
            send(ahead, ahead, relay_send.at[i, 0], relay_recv.at[i, 0], line(1 - h, 1)),
            send(back, back, relay_send.at[i, 1], relay_recv.at[i, 1], line(1 - h, 3)),
        ])

    for copy in turns:
        copy.wait_recv()
    sent += turns
    behind, before = shifted(y, 3) * 2 + core, shifted(y, 1) * 2 + core
    low, high = pl.ds(0, HOSTS // 2), pl.ds(HOSTS // 2, HOSTS // 2)
    onward = [
        send(heads.at[behind, low], heads.at[behind, low], dp_send.at[2], dp_recv.at[2], along_y(1)),
        send(heads.at[before, high], heads.at[before, high], dp_send.at[3], dp_recv.at[3], along_y(3)),
    ]
    swaps += [
        send(heads.at[g], heads.at[g], core_send.at[n], core_recv.at[n], partner)
        for n, g in ((1, behind), (2, before))
    ]
    for copy in onward:
        copy.wait_recv()
    sent += onward
    across = shifted(y, 2) * 2 + core
    swaps.append(send(heads.at[across], heads.at[across], core_send.at[3], core_recv.at[3], partner))
    for copy in swaps:
        copy.wait_recv()
    sent += swaps

    def unpack(n, carry):
        at = n // SIDE
        first = n % SIDE * SIDE
        block = heads[at, pl.ds(first, SIDE)].astype(jnp.float32)
        queries, latents = [], []
        for t in range(SIDE):
            queries.append(jnp.concatenate(
                [block[t, g * qrows : (g + 1) * qrows] for g in range(qgroups)], axis=1))
            base = qgroups * qrows
            latents.append(jnp.concatenate(
                [block[t, base + g * lrows : base + (g + 1) * lrows] for g in range(lgroups)], axis=1))
        to_q = pl.ds(pl.multiple_of(n * SIDE * qrows, 16), SIDE * qrows)
        to_l = pl.ds(pl.multiple_of(n * SIDE * lrows, 16), SIDE * lrows)
        query_rows[to_q, :] = jnp.concatenate(queries, axis=0).astype(jnp.bfloat16)
        latent_rows[to_l, :] = jnp.concatenate(latents, axis=0).astype(jnp.bfloat16)
        return carry

    lax.fori_loop(0, 2 * SIDE * SIDE, unpack, 0)
    for n, (src, dst) in enumerate(((query_rows, query_out), (latent_rows, latent_out))):
        copy = pltpu.make_async_copy(src, dst, head_store.at[n])
        copy.start()
        kept.append(copy)

    def place(h, d, s):
        u, v = coords(h)
        wanted = slots_of[s, host(h, shifted(u, d), v)]
        found = 0
        for p in range(HOSTS):
            kept_at = p if h == 0 else p % SIDE * SIDE + p // SIDE
            found = jnp.where(expert_of[p] == wanted, kept_at, found)
        return found, wanted >= 0

    places = {(h, d, s): place(h, d, s) for h in range(2) for d in range(SIDE) for s in range(slots_of.shape[0])}

    delivered = []
    for k in range(SPLITS):
        for h in range(2):
            i = 2 * k + h
            for copy in relays[i]:
                copy.wait_recv()
            sent += relays[i]
            for d in (1, 3, 2, 0):
                for s in range(slots_of.shape[0]):
                    found, filled = places[h, d, s]
                    block = gathered[i][found]
                    staged[i, d, s] = jnp.where(filled, block, jnp.zeros_like(block))
        for h in range(2):
            i = 2 * k + h
            u, v = coords(h)
            window = expert_out.at[
                :, pl.ds(pl.multiple_of(half * h + u * part, 16), part), pl.ds(cols * k, cols)
            ]
            delivered += [
                send(staged.at[i, d], window, deliver_send.at[i, d - 1], deliver_recv.at[i, d - 1], line(h, d))
                for d in (1, 3, 2)
            ]
            copy = pltpu.make_async_copy(staged.at[i, 0], window, keep_sem.at[i])
            copy.start()
            kept.append(copy)

    for copy in kept:
        copy.wait()
    for copy in delivered:
        copy.wait_recv()
    for copy in sent + delivered:
        copy.wait_send()


def per_device(
    query_weight, query_state, latent_weight, latent_state, expert_weight, expert_state,
    decay, shard_expert, host_slots,
):
    groups = lax.axis_size("dp")
    rows, width = expert_weight.shape[1:]
    slots = host_slots.shape[1]
    half, cols = rows // 2, width // SPLITS
    part = half // SIDE
    count = len(PIECES)
    qrows, qwidth = query_weight.shape
    lrows, lwidth = latent_weight.shape
    qcols, lcols = qwidth // HOSTS, lwidth // HOSTS
    packed_rows = pl.cdiv(qrows * qcols // LANES + lrows * lcols // LANES, 16) * 16
    bf16, f32 = jnp.bfloat16, jnp.float32
    vmem, dma = pltpu.VMEM, pltpu.SemaphoreType.DMA
    hop = SIDE - 1
    anywhere = pl.BlockSpec(memory_space=pl.ANY)
    query_serving, latent_serving, expert_serving = pl.pallas_call(
        kernel,
        name="publish_exchange",
        out_shape=(
            jax.ShapeDtypeStruct((groups * HOSTS * qrows, qcols), bf16),
            jax.ShapeDtypeStruct((groups * HOSTS * lrows, lcols), bf16),
            jax.ShapeDtypeStruct((slots, rows, width), bf16),
        ),
        in_specs=[pl.BlockSpec(memory_space=pltpu.HBM)] * 9,
        out_specs=(anywhere,) * 3,
        scratch_shapes=[
            pltpu.SMEM(shard_expert.shape, jnp.int32),
            pltpu.SMEM(host_slots.shape[::-1], jnp.int32),
            pltpu.SMEM(decay.shape, f32),
            dma((3,)),
            vmem((qrows, qwidth), bf16),
            vmem((qrows, qwidth), f32),
            vmem((lrows, lwidth), bf16),
            vmem((lrows, lwidth), f32),
            vmem((SIDE, SIDE, packed_rows, LANES), bf16),
            vmem((SIDE, SIDE, packed_rows, LANES), bf16),
            vmem((groups, HOSTS, packed_rows, LANES), bf16),
            vmem((groups * HOSTS * qrows, qcols), bf16),
            vmem((groups * HOSTS * lrows, lcols), bf16),
            vmem((LOADED, half, cols), bf16),
            vmem((LOADED, half, cols), f32),
            vmem((count, half, cols), bf16),
            vmem((count, SIDE, slots, part, cols), bf16),
        ]
        + [vmem((HOSTS, part, cols), bf16)] * count
        + [
            dma((4,)), dma((2,)),
            dma((hop,)), dma((hop,)), dma, dma((hop,)), dma((hop,)), dma,
            dma((4,)), dma((4,)), dma((4,)), dma((4,)),
            dma((count, 2)), dma((count,)),
            dma((count, hop)), dma((count, hop)),
            dma((count, 2)), dma((count, 2)), dma((count, 2)), dma((count, 2)),
            dma((count, hop)), dma((count, hop)), dma((count,)),
        ],
        compiler_params=pltpu.CompilerParams(
            collective_id=0, has_side_effects=True, vmem_limit_bytes=42 * 2**20
        ),
    )(
        *(
            pltpu.with_memory_space_constraint(a, pltpu.HBM)
            for a in (
                shard_expert, host_slots.T, decay, query_weight, query_state, latent_weight, latent_state, expert_weight[0], expert_state[0],
            )
        ),
    )
    return query_serving, latent_serving, expert_serving[None]


def solution(mesh):
    placed = (
        P(("dp", "tensor"), None),
        P(("dp", "tensor"), None),
        P(("dp", "tensor"), None),
        P(("dp", "tensor"), None),
        P("tensor", "dp", None),
        P("tensor", "dp", None),
        P(),
        P(),
        P(),
    )
    return jax.shard_map(
        per_device,
        mesh=mesh,
        in_specs=placed,
        out_specs=(P(None, "tensor"), P(None, "tensor"), P("tensor", None, "dp", None)),
        check_vma=False,
    )
```

time: 229 us -> 139 us (0.61)
  waiting for transfers between devices: 155 us -> 0 us
  Pallas kernels: 0 us -> 133 us
  starting transfers between devices: 24.5 us -> 0 us
  between operations: 16.1 us -> 0.64 us
  other arithmetic: 15.4 us -> 0 us
  local copies, waits for them, and re-layouts: 16.9 us -> 5.42 us
    pallas_call x0 -> x1, Pallas kernels: none -> 133 us  [per_device(): pl.pallas_call(kernel, name='publish_exchange', out_shape=(jax.ShapeDtype...]
    all_to_all x4 -> x0, waiting for transfers between devices: 101 us -> none  [the longest x1 51.3 us: per_device(): lax.all_to_all(blended.reshape(host_count, chunk, width), 'tensor', split...]
    all_gather x2 -> x0, waiting for transfers between devices: 53.9 us -> none  [serve_columns(): lax.all_gather(moved.reshape(host_count * rows, width // host_count), 'dp...]
    all_to_all x4 -> x0, starting transfers between devices: 24.4 us -> none  [the longest x2 12.3 us: serve_columns(): lax.all_to_all(split, 'tensor', split_axis=0, concat_axis=0, tiled=True)]
    convert_element_type x3 -> x0, other arithmetic: 11.3 us -> none  [publish(): (rate * state_part + (1.0 - rate) * weight_part.astype(jnp.float32)).asty...]
    gather x1 -> x0, local copies, waits for them, and re-layouts: 6.1 us -> none  [per_device(): spread[stored.reshape(-1)]]
    transpose x1 -> x0, local copies, waits for them, and re-layouts: 4.46 us -> none  [per_device(): received.transpose(1, 0, 2, 3).reshape(1, host_slots.shape[1], rows, width)]
    select_n x2 -> x0, other arithmetic: 3.6 us -> none  [the longest x1 3.59 us: per_device(): jnp.where(own_filled[None, :, None, None], slots, jnp.zeros_like(slots))]
  transfers between devices with their start and end apart: 6 -> 0, of which waited for: 5 -> 0; matrix products, arithmetic and copies ran while one was open for 8% -> 0% of each run, Pallas kernels for 0% -> 0%
where the time goes in v3:
time: 139 us
  Pallas kernels  133 us (96%)
  local copies, waits for them, and re-layouts  5.42 us (4%)
    pallas_call x1, Pallas kernels, per_device(): pl.pallas_call(kernel, name='publish_exchange', out_shape=(jax.ShapeDtype...  133 us
    unnamed x3, local copies, waits for them, and re-layouts  5.42 us

profile of v3, /device:TPU:0, one launch (start us, length us, event | category | flops | bytes accessed | tf_op | source)
XLA Modules:
  0.0 139.0 jit_solution(2358470212848388748)
XLA Ops:
  0.6 133.0 %publish_exchange.1 = (bf16[1536,768]{1,0:T(8,128)(2,1)S(1)}, bf16[512,1024]{1,0:T(8,128)(2,1)S(1)}, bf16[2,896,2048]{2,1,0:T(8,128)(2,1)S(1)}) custom-call(s32[16]{0:T(128)} %expert_table.1, s32[2,16]{1,0:T(2,128)} %bitcast.7, f32[3]{0:T(128)} %decay_table.1, bf16[12,12288]{1,0:T(8,128)(2,1)} %query_weight.1, f32[12,12288]{1,0:T(8,128)} %query_state.1, ...), custom_call_target="tpu_custom_call" | custom-call | tf_op jit(solution)/shard_map/publish_exchange/pallas_call | solution.py:337
  133.6 1.4 %copy.15 = bf16[1536,768]{1,0:T(8,128)(2,1)} copy(bf16[1536,768]{1,0:T(8,128)(2,1)S(1)} %get-tuple-element.12) | data formatting | bytes 4718592
  135.0 1.0 copy.16
  136.0 3.0 %copy.17 = bf16[1,2,896,2048]{3,2,1,0:T(8,128)(2,1)} copy(bf16[1,2,896,2048]{3,2,1,0:T(8,128)(2,1)S(1)} %bitcast.4) | data formatting | bytes 14680064

commit v4 on v3

--- a/solution.py
+++ b/solution.py
@@ -1,3 +1,5 @@
+import functools
+
 import jax
 import jax.numpy as jnp
 from jax import lax
@@ -12,6 +14,9 @@
 PIECES = tuple((h, k) for k in range(SPLITS) for h in range(2))
 LOADED = 4
 LANES = 128
+ROUND = 2
+CODES = 4 * ROUND + HOSTS
+HELD = 2 * SIDE * CODES
 
 
 def publish(weight, state, rate):
@@ -31,19 +36,125 @@
     return copy
 
 
+def ring_place(h, p):
+    return (p % SIDE, p // SIDE) if h == 0 else (p // SIDE, p % SIDE)
+
+
+def code_at(h, v, n):
+    return (h * SIDE + v) * CODES + n
+
+
+def router(expert_of, slots_of, route, fits, need):
+    def held_by(e):
+        return route[HELD + jnp.clip(e, 0, HOSTS - 1)]
+
+    for p in range(HOSTS):
+        route[HELD + jnp.clip(expert_of[p], 0, HOSTS - 1)] = p
+        need[0, p] = 0
+        need[1, p] = 0
+    for t in range(HOSTS):
+        for s in range(slots_of.shape[0]):
+            e = slots_of[s, t]
+            p = held_by(e)
+            for h in range(2):
+                need[h, p] = need[h, p] | jnp.where(e >= 0, 1 << ring_place(h, t)[1], 0)
+
+    good = jnp.bool_(True)
+    for h in range(2):
+        own = [[0, 0] for _ in range(SIDE)]
+        far = [[0, 0] for _ in range(SIDE)]
+        passing = [[0, 0] for _ in range(SIDE)]
+        wants = []
+        for p in range(HOSTS):
+            _, v = ring_place(h, p)
+            rows = need[h, p]
+            near = [(rows >> shifted(v, 1)) & 1, (rows >> shifted(v, 3)) & 1]
+            across = (rows >> shifted(v, 2)) & 1
+            wants.append((near, across))
+            for way in range(2):
+                own[v][way] = own[v][way] + near[way]
+        ways = []
+        for p in range(HOSTS):
+            _, v = ring_place(h, p)
+            near, across = wants[p]
+            price = []
+            for way, d in enumerate((1, 3)):
+                fresh = 1 - near[way]
+                after = shifted(v, d)
+                mine = 2 * (own[v][way] + passing[v][way] + fresh) + jnp.where(far[v][way] >= ROUND, 100, 0)
+                theirs = 2 * (own[after][way] + passing[after][way] + 1)
+                price.append(jnp.maximum(mine, theirs) + fresh)
+            forward = (price[0] <= price[1]).astype(jnp.int32)
+            hop = [across * forward, across * (1 - forward)]
+            ways.append(hop)
+            for way, d in enumerate((1, 3)):
+                after = shifted(v, d)
+                own[v][way] = own[v][way] + hop[way] * (1 - near[way])
+                far[v][way] = far[v][way] + hop[way]
+                passing[after][way] = passing[after][way] + hop[way]
+        places = [[ring_place(h, p)[0] if ring_place(h, p)[1] == v else 0 for p in range(HOSTS)] for v in range(SIDE)]
+        sends = [[0] * (4 * ROUND) for _ in range(SIDE)]
+        for v in range(SIDE):
+            for way, d in enumerate((1, 3)):
+                late = jnp.maximum(own[v][way] - ROUND, 0)
+                good = good & (far[v][way] <= ROUND) & (late + passing[v][way] <= ROUND)
+                after, last = shifted(v, d), shifted(v, 2)
+                onward = jnp.maximum(own[after][way] - ROUND, 0)
+                mine = [p for p in range(HOSTS) if ring_place(h, p)[1] == v]
+                at = 0
+                spots = {}
+                for p in mine:
+                    spots[p] = at
+                    at = at + ways[p][way]
+                for p in mine:
+                    near, _ = wants[p]
+                    only = near[way] * (1 - ways[p][way])
+                    spots[p] = jnp.where(only == 1, at, spots[p])
+                    at = at + only
+                hops = 0
+                for p in mine:
+                    near, _ = wants[p]
+                    sent = (near[way] | ways[p][way]) == 1
+                    spot = spots[p]
+                    for n in range(2 * ROUND):
+                        entry = (n // ROUND) * 2 * ROUND + way * ROUND + n % ROUND
+                        sends[v][entry] = jnp.where(sent & (spot == n), ring_place(h, p)[0], sends[v][entry])
+                    landed = way * ROUND + jnp.where(spot < ROUND, 4 + spot, 8 + spot - ROUND)
+                    places[after][p] = jnp.where(near[way] == 1, landed, places[after][p])
+                    goes = ways[p][way] == 1
+                    turn = onward + hops
+                    for n in range(ROUND):
+                        entry = 2 * ROUND + way * ROUND + n
+                        sends[after][entry] = jnp.where(goes & (turn == n), 4 + way * ROUND + spot, sends[after][entry])
+                    places[last][p] = jnp.where(goes, 8 + way * ROUND + turn, places[last][p])
+                    hops = hops + ways[p][way]
+        for v in range(SIDE):
+            for n in range(4 * ROUND):
+                route[code_at(h, v, n)] = sends[v][n]
+            for p in range(HOSTS):
+                route[code_at(h, v, 4 * ROUND + p)] = places[v][p]
+    fits[0] = good.astype(jnp.int32)
+
+
 def kernel(
-    expert_table, slot_table, decay_table,
+    routed, route_table, slot_table, decay_table,
     query_weight, query_state, latent_weight, latent_state, expert_weight, expert_state,
     query_out, latent_out, expert_out,
-    expert_of, slots_of, decay, table_sem, qw, qs, lw, ls, packed, crossed, heads, query_rows, latent_rows,
-    wbuf, sbuf, own, staged, *rest,
+    route, slots_of, decay, table_sem, qw, qs, lw, ls, packed, crossed, heads, query_rows, latent_rows,
+    sbuf, own, staged, *rest,
 ):
     count = len(PIECES)
-    gathered = rest[:count]
+    if routed:
+        first_out, second_out = rest[:2]
+        first, second = rest[2 + count : 2 + 2 * count], rest[2 + 2 * count : 2 + 3 * count]
+        gathered = rest[2 : 2 + count]
+        rest = rest[2 + 3 * count :]
+    else:
+        gathered, rest = rest[:count], rest[count:]
     (head_load, head_store, cross_send, cross_recv, cross_keep, column_send, column_recv, column_keep,
      dp_send, dp_recv, core_send, core_recv,
      load_sem, local_sem, spread_send, spread_recv, ring_send, ring_recv, relay_send, relay_recv,
-     deliver_send, deliver_recv, keep_sem) = rest[count:]
+     deliver_send, deliver_recv, keep_sem) = rest
 
     rows, width = expert_weight.shape
     half, cols = rows // 2, width // SPLITS
@@ -82,7 +193,7 @@
     tables = [
         pltpu.make_async_copy(src, dst, table_sem.at[n])
         for n, (src, dst) in enumerate(
-            ((expert_table, expert_of), (slot_table, slots_of), (decay_table, decay))
+            ((route_table, route), (slot_table, slots_of), (decay_table, decay))
         )
     ]
     for copy in tables:
@@ -91,7 +202,7 @@
     for i, (h, k) in enumerate(PIECES):
         window = (pl.ds(half * h, half), pl.ds(cols * k, cols))
         loads.append((
-            pltpu.make_async_copy(expert_weight.at[window], wbuf.at[i % LOADED], load_sem.at[i, 0]),
+            pltpu.make_async_copy(expert_weight.at[window], own.at[i], load_sem.at[i, 0]),
             pltpu.make_async_copy(expert_state.at[window], sbuf.at[i % LOADED], load_sem.at[i, 1]),
         ))
 
@@ -119,7 +230,7 @@
 
         def body(r, carry):
             at = pl.ds(pl.multiple_of(r * step, step), step)
-            own[i, at, :] = publish(wbuf[i % LOADED, at, :], sbuf[i % LOADED, at, :], decay[2]).astype(jnp.bfloat16)
+            own[i, at, :] = publish(own[i, at, :], sbuf[i % LOADED, at, :], decay[2]).astype(jnp.bfloat16)
             return carry
 
         lax.fori_loop(0, half // step, body, 0)
@@ -135,7 +246,7 @@
     def spread(i):
         h, _ = PIECES[i]
         u, v = coords(h)
-        mine = v * SIDE + u
+        mine = u if routed else v * SIDE + u
         copies = [
             send(own.at[i, row_part(shifted(u, d))], gathered[i].at[mine], spread_send.at[i, d - 1],
                  spread_recv.at[i, d - 1], line(h, d))
@@ -191,19 +302,49 @@
     )
     column_local.start()
 
+    def pick(code, *stores):
+        block = stores[0][jnp.clip(code, 0, SIDE - 1)]
+        for n, store in enumerate(stores[1:], 1):
+            later = store[jnp.clip(code - n * SIDE, 0, SIDE - 1)]
+            block = jnp.where(code >= n * SIDE, later, block)
+        return block
+
+    def routed_round(i, n, out, into, stores, send_sem, recv_sem):
+        h, _ = PIECES[i]
+        _, v = coords(h)
+        for way in range(2):
+            for j in range(ROUND):
+                out[i, way, j] = pick(route[code_at(h, v, n * 2 * ROUND + way * ROUND + j)], *stores)
+
+        def go():
+            return [
+                send(out.at[i, way], into.at[pl.ds(way * ROUND, ROUND)], send_sem.at[i, way],
+                     recv_sem.at[i, way], line(1 - h, d))
+                for way, d in enumerate((1, 3))
+            ]
+
+        return go
+
     rings = []
-    for i, (h, k) in enumerate(PIECES):
-        u, v = coords(h)
-        copies, local = spreads[i]
-        for copy in copies:
-            copy.wait_recv()
-        local.wait()
-        sent += copies
-        line_blocks = gathered[i].at[pl.ds(v * SIDE, SIDE)]
-        rings.append([
-            send(line_blocks, line_blocks, ring_send.at[i, n], ring_recv.at[i, n], line(1 - h, d))
-            for n, d in enumerate((1, 3))
-        ])
+    for k in range(SPLITS):
+        starts = []
+        for h in range(2):
+            i = 2 * k + h
+            u, v = coords(h)
+            copies, local = spreads[i]
+            for copy in copies:
+                copy.wait_recv()
+            local.wait()
+            sent += copies
+            if routed:
+                starts.append(routed_round(i, 0, first_out, first[i], gathered[i : i + 1], ring_send, ring_recv))
+            else:
+                line_blocks = gathered[i].at[pl.ds(v * SIDE, SIDE)]
+                rings.append([
+                    send(line_blocks, line_blocks, ring_send.at[i, n], ring_recv.at[i, n], line(1 - h, d))
+                    for n, d in enumerate((1, 3))
+                ])
+        rings += [go() for go in starts]
 
     for copy in columns:
         copy.wait_recv()
@@ -214,17 +355,25 @@
     swaps = [send(mine, mine, core_send.at[0], core_recv.at[0], partner)]
 
     relays = []
-    for i, (h, k) in enumerate(PIECES):
-        u, v = coords(h)
-        for copy in rings[i]:
-            copy.wait_recv()
-        sent += rings[i]
-        ahead = gathered[i].at[pl.ds(shifted(v, 3) * SIDE, SIDE // 2)]
-        back = gathered[i].at[pl.ds(shifted(v, 1) * SIDE + SIDE // 2, SIDE // 2)]
-        relays.append([
-            send(ahead, ahead, relay_send.at[i, 0], relay_recv.at[i, 0], line(1 - h, 1)),
-            send(back, back, relay_send.at[i, 1], relay_recv.at[i, 1], line(1 - h, 3)),
-        ])
+    for k in range(SPLITS):
+        starts = []
+        for h in range(2):
+            i = 2 * k + h
+            u, v = coords(h)
+            for copy in rings[i]:
+                copy.wait_recv()
+            sent += rings[i]
+            if routed:
+                starts.append(routed_round(
+                    i, 1, second_out, second[i], (gathered[i], first[i]), relay_send, relay_recv))
+            else:
+                ahead = gathered[i].at[pl.ds(shifted(v, 3) * SIDE, SIDE // 2)]
+                back = gathered[i].at[pl.ds(shifted(v, 1) * SIDE + SIDE // 2, SIDE // 2)]
+                relays.append([
+                    send(ahead, ahead, relay_send.at[i, 0], relay_recv.at[i, 0], line(1 - h, 1)),
+                    send(back, back, relay_send.at[i, 1], relay_recv.at[i, 1], line(1 - h, 3)),
+                ])
+        relays += [go() for go in starts]
 
     for copy in turns:
         copy.wait_recv()
@@ -274,10 +423,11 @@
     def place(h, d, s):
         u, v = coords(h)
         wanted = slots_of[s, host(h, shifted(u, d), v)]
-        found = 0
-        for p in range(HOSTS):
-            kept_at = p if h == 0 else p % SIDE * SIDE + p // SIDE
-            found = jnp.where(expert_of[p] == wanted, kept_at, found)
+        p = jnp.clip(route[HELD + jnp.clip(wanted, 0, HOSTS - 1)], 0, HOSTS - 1)
+        if routed:
+            found = route[code_at(h, v, 4 * ROUND + p)]
+        else:
+            found = p if h == 0 else p % SIDE * SIDE + p // SIDE
         return found, wanted >= 0
 
     places = {(h, d, s): place(h, d, s) for h in range(2) for d in range(SIDE) for s in range(slots_of.shape[0])}
@@ -292,7 +442,10 @@
             for d in (1, 3, 2, 0):
                 for s in range(slots_of.shape[0]):
                     found, filled = places[h, d, s]
-                    block = gathered[i][found]
+                    if routed:
+                        block = pick(found, gathered[i], first[i], second[i])
+                    else:
+                        block = gathered[i][found]
                     staged[i, d, s] = jnp.where(filled, block, jnp.zeros_like(block))
         for h in range(2):
             i = 2 * k + h
@@ -334,55 +487,76 @@
     vmem, dma = pltpu.VMEM, pltpu.SemaphoreType.DMA
     hop = SIDE - 1
     anywhere = pl.BlockSpec(memory_space=pl.ANY)
-    query_serving, latent_serving, expert_serving = pl.pallas_call(
-        kernel,
-        name="publish_exchange",
+    smem = pl.BlockSpec(memory_space=pltpu.SMEM)
+    in_hbm = functools.partial(pltpu.with_memory_space_constraint, memory_space=pltpu.HBM)
+    route, fits = pl.pallas_call(
+        router,
+        name="router",
         out_shape=(
-            jax.ShapeDtypeStruct((groups * HOSTS * qrows, qcols), bf16),
-            jax.ShapeDtypeStruct((groups * HOSTS * lrows, lcols), bf16),
-            jax.ShapeDtypeStruct((slots, rows, width), bf16),
+            jax.ShapeDtypeStruct((HELD + HOSTS,), jnp.int32),
+            jax.ShapeDtypeStruct((1,), jnp.int32),
         ),
-        in_specs=[pl.BlockSpec(memory_space=pltpu.HBM)] * 9,
-        out_specs=(anywhere,) * 3,
-        scratch_shapes=[
-            pltpu.SMEM(shard_expert.shape, jnp.int32),
-            pltpu.SMEM(host_slots.shape[::-1], jnp.int32),
-            pltpu.SMEM(decay.shape, f32),
-            dma((3,)),
-            vmem((qrows, qwidth), bf16),
-            vmem((qrows, qwidth), f32),
-            vmem((lrows, lwidth), bf16),
-            vmem((lrows, lwidth), f32),
-            vmem((SIDE, SIDE, packed_rows, LANES), bf16),
-            vmem((SIDE, SIDE, packed_rows, LANES), bf16),
-            vmem((groups, HOSTS, packed_rows, LANES), bf16),
-            vmem((groups * HOSTS * qrows, qcols), bf16),
-            vmem((groups * HOSTS * lrows, lcols), bf16),
-            vmem((LOADED, half, cols), bf16),
-            vmem((LOADED, half, cols), f32),
-            vmem((count, half, cols), bf16),
-            vmem((count, SIDE, slots, part, cols), bf16),
-        ]
-        + [vmem((HOSTS, part, cols), bf16)] * count
-        + [
-            dma((4,)), dma((2,)),
-            dma((hop,)), dma((hop,)), dma, dma((hop,)), dma((hop,)), dma,
-            dma((4,)), dma((4,)), dma((4,)), dma((4,)),
-            dma((count, 2)), dma((count,)),
-            dma((count, hop)), dma((count, hop)),
-            dma((count, 2)), dma((count, 2)), dma((count, 2)), dma((count, 2)),
-            dma((count, hop)), dma((count, hop)), dma((count,)),
-        ],
-        compiler_params=pltpu.CompilerParams(
-            collective_id=0, has_side_effects=True, vmem_limit_bytes=42 * 2**20
-        ),
-    )(
-        *(
-            pltpu.with_memory_space_constraint(a, pltpu.HBM)
-            for a in (
-                shard_expert, host_slots.T, decay, query_weight, query_state, latent_weight, latent_state, expert_weight[0], expert_state[0],
-            )
-        ),
+        in_specs=[smem] * 2,
+        out_specs=(smem,) * 2,
+        scratch_shapes=[pltpu.SMEM((2, HOSTS), jnp.int32)],
+    )(shard_expert, host_slots.T)
+
+    def exchange(routed, *operands):
+        block = vmem((SIDE, part, cols), bf16)
+        outgoing = vmem((count, 2, ROUND, part, cols), bf16)
+        if routed:
+            stores = [outgoing] * 2 + [block] * (3 * count)
+        else:
+            stores = [vmem((HOSTS, part, cols), bf16)] * count
+        return pl.pallas_call(
+            functools.partial(kernel, routed),
+            name="routed_exchange" if routed else "full_exchange",
+            out_shape=(
+                vmem((groups * HOSTS * qrows, qcols), bf16),
+                vmem((groups * HOSTS * lrows, lcols), bf16),
+                vmem((slots, rows, width), bf16),
+            ),
+            in_specs=[pl.BlockSpec(memory_space=pltpu.HBM)] * 9,
+            out_specs=(anywhere,) * 3,
+            scratch_shapes=[
+                pltpu.SMEM(route.shape, jnp.int32),
+                pltpu.SMEM(host_slots.shape[::-1], jnp.int32),
+                pltpu.SMEM(decay.shape, f32),
+                dma((3,)),
+                vmem((qrows, qwidth), bf16),
+                vmem((qrows, qwidth), f32),
+                vmem((lrows, lwidth), bf16),
+                vmem((lrows, lwidth), f32),
+                vmem((SIDE, SIDE, packed_rows, LANES), bf16),
+                vmem((SIDE, SIDE, packed_rows, LANES), bf16),
+                vmem((groups, HOSTS, packed_rows, LANES), bf16),
+                vmem((groups * HOSTS * qrows, qcols), bf16),
+                vmem((groups * HOSTS * lrows, lcols), bf16),
+                vmem((LOADED, half, cols), f32),
+                vmem((count, half, cols), bf16),
+                vmem((count, SIDE, slots, part, cols), bf16),
+            ]
+            + stores
+            + [
+                dma((4,)), dma((2,)),
+                dma((hop,)), dma((hop,)), dma, dma((hop,)), dma((hop,)), dma,
+                dma((4,)), dma((4,)), dma((4,)), dma((4,)),
+                dma((count, 2)), dma((count,)),
+                dma((count, hop)), dma((count, hop)),
+                dma((count, 2)), dma((count, 2)), dma((count, 2)), dma((count, 2)),
+                dma((count, hop)), dma((count, hop)), dma((count,)),
+            ],
+            compiler_params=pltpu.CompilerParams(
+                collective_id=0 if routed else 1, has_side_effects=True, vmem_limit_bytes=43 * 2**20
+            ),
+        )(*(in_hbm(a) for a in operands))
+
+    query_serving, latent_serving, expert_serving = lax.cond(
+        fits[0] == 1,
+        functools.partial(exchange, True),
+        functools.partial(exchange, False),
+        route, host_slots.T, decay,
+        query_weight, query_state, latent_weight, latent_state, expert_weight[0], expert_state[0],
     )
     return query_serving, latent_serving, expert_serving[None]
 

time: 139 us -> 123 us (0.88)
  Pallas kernels: 133 us -> 116 us
    pallas_call x1 -> x2, Pallas kernels: 133 us -> 116 us  [the longest x1 113 us: exchange(): pl.pallas_call(functools.partial(kernel, routed), name='routed_exchange'...]
where the time goes in v4:
time: 123 us
  Pallas kernels  116 us (94%)
  local copies, waits for them, and re-layouts  5.42 us (4%)
  between operations  1.3 us (1%)
    pallas_call x1, Pallas kernels, exchange(): pl.pallas_call(functools.partial(kernel, routed), name='routed_exchange'...  113 us
    unnamed x3, local copies, waits for them, and re-layouts  5.42 us
    pallas_call x1, Pallas kernels, per_device(): pl.pallas_call(router, name='router', out_shape=(jax.ShapeDtypeStruct((HE...  3.01 us

profile of v4, /device:TPU:0, one launch (start us, length us, event | category | flops | bytes accessed | tf_op | source)
XLA Modules:
  0.0 123.1 jit_solution(16815079113880773611)
XLA Ops:
  0.6 3.0 %router.1 = (s32[208]{0:T(256)}, s32[1]{0:T(128)}) custom-call(s32[16]{0:T(128)} %expert_of.1, s32[2,16]{1,0:T(2,128)} %bitcast.12), custom_call_target="tpu_custom_call" | custom-call | tf_op jit(solution)/shard_map/router/pallas_call | solution.py:492
  4.3 113.3 %conditional.1 = (bf16[1536,768]{1,0:T(8,128)(2,1)S(1)}, bf16[512,1024]{1,0:T(8,128)(2,1)S(1)}, bf16[1,2,896,2048]{3,2,1,0:T(8,128)(2,1)S(1)}) conditional(s32[]{:T(128)} %bitcast.3, (s32[208]{0:T(256)}, s32[2,16]{1,0:T(2,128)}, f32[3]{0:T(128)}, bf16[12,12288]{1,0:T(8,128)(2,1)}, f32[12,12288]{1,0:T(8,128)}, /*index=5*/bf16[4,16384]{1,0:T(4,128)(2,1)}, ...), branch_computations={%region_0.0_spmd, %region_1.0_spmd} | conditional | bytes 24 | solution.py:554
  4.3 113.3 %routed_exchange.1 = (bf16[1536,768]{1,0:T(8,128)(2,1)S(1)}, bf16[512,1024]{1,0:T(8,128)(2,1)S(1)}, bf16[2,896,2048]{2,1,0:T(8,128)(2,1)S(1)}) custom-call(s32[208]{0:T(256)} %get-tuple-element.55.route_table, s32[2,16]{1,0:T(2,128)} %get-tuple-element.56.slot_table, f32[3]{0:T(128)} %get-tuple-element.57.decay_table, ...), custom_call_target="tpu_custom_call" | custom-call | tf_op jit(solution)/shard_map/cond/branch_1_fun/routed_exchange/pallas_call | solution.py:511
  117.6 1.4 %copy.23 = bf16[1536,768]{1,0:T(8,128)(2,1)} copy(bf16[1536,768]{1,0:T(8,128)(2,1)S(1)} %get-tuple-element.81) | data formatting | bytes 4718592
  119.0 1.0 copy.24
  120.0 3.0 %copy.25 = bf16[1,2,896,2048]{3,2,1,0:T(8,128)(2,1)} copy(bf16[1,2,896,2048]{3,2,1,0:T(8,128)(2,1)S(1)} %get-tuple-element.83) | data formatting | bytes 14680064

commit v5 on v4

--- a/solution.py
+++ b/solution.py
@@ -469,6 +469,18 @@
         copy.wait_send()
 
 
+def settle(query_in, latent_in, expert_in, query_out, latent_out, expert_out, sems):
+    pairs = [(latent_in, latent_out)]
+    for src, dst in ((query_in, query_out), (expert_in.at[0], expert_out.at[0]), (expert_in.at[1], expert_out.at[1])):
+        half = src.shape[0] // 2
+        pairs += [(src.at[pl.ds(half * n, half)], dst.at[pl.ds(half * n, half)]) for n in range(2)]
+    copies = [pltpu.make_async_copy(src, dst, sems.at[n]) for n, (src, dst) in enumerate(pairs)]
+    for copy in copies:
+        copy.start()
+    for copy in copies:
+        copy.wait()
+
+
 def per_device(
     query_weight, query_state, latent_weight, latent_state, expert_weight, expert_state,
     decay, shard_expert, host_slots,
@@ -508,7 +520,7 @@
             stores = [outgoing] * 2 + [block] * (3 * count)
         else:
             stores = [vmem((HOSTS, part, cols), bf16)] * count
-        return pl.pallas_call(
+        results = pl.pallas_call(
             functools.partial(kernel, routed),
             name="routed_exchange" if routed else "full_exchange",
             out_shape=(
@@ -550,6 +562,15 @@
                 collective_id=0 if routed else 1, has_side_effects=True, vmem_limit_bytes=43 * 2**20
             ),
         )(*(in_hbm(a) for a in operands))
+        return pl.pallas_call(
+            settle,
+            name="settle",
+            out_shape=tuple(jax.ShapeDtypeStruct(a.shape, bf16) for a in results),
+            in_specs=[anywhere] * 3,
+            out_specs=(anywhere,) * 3,
+            scratch_shapes=[dma((7,))],
+            compiler_params=pltpu.CompilerParams(vmem_limit_bytes=2**20),
+        )(*(pltpu.with_memory_space_constraint(a, pltpu.VMEM) for a in results))
 
     query_serving, latent_serving, expert_serving = lax.cond(
         fits[0] == 1,

time: 123 us -> 122 us (level)
  local copies, waits for them, and re-layouts: 5.42 us -> 0 us
  Pallas kernels: 116 us -> 120 us
    unnamed x3 -> x0, local copies, waits for them, and re-layouts: 5.42 us -> none
    pallas_call x0 -> x1, Pallas kernels: none -> 4.12 us  [exchange(): pl.pallas_call(settle, name='settle', out_shape=tuple((jax.ShapeDtypeStru...]
where the time goes in v5:
time: 122 us
  Pallas kernels  120 us (98%)
  between operations  1.29 us (1%)
    pallas_call x1, Pallas kernels, exchange(): pl.pallas_call(functools.partial(kernel, routed), name='routed_exchange'...  113 us
    pallas_call x1, Pallas kernels, exchange(): pl.pallas_call(settle, name='settle', out_shape=tuple((jax.ShapeDtypeStru...  4.12 us
    pallas_call x1, Pallas kernels, per_device(): pl.pallas_call(router, name='router', out_shape=(jax.ShapeDtypeStruct((HE...  3.01 us

profile of v5, /device:TPU:0, one launch (start us, length us, event | category | flops | bytes accessed | tf_op | source)
XLA Modules:
  0.0 121.8 jit_solution(8897934524748247098)
XLA Ops:
  0.6 3.0 %router.1 = (s32[208]{0:T(256)}, s32[1]{0:T(128)}) custom-call(s32[16]{0:T(128)} %expert_of.1, s32[2,16]{1,0:T(2,128)} %bitcast.10), custom_call_target="tpu_custom_call" | custom-call | tf_op jit(solution)/shard_map/router/pallas_call | solution.py:504
  4.3 117.5 %conditional.1 = (bf16[1536,768]{1,0:T(8,128)(2,1)}, bf16[512,1024]{1,0:T(8,128)(2,1)}, bf16[1,2,896,2048]{3,2,1,0:T(8,128)(2,1)}) conditional(s32[]{:T(128)} %bitcast.3, (s32[208]{0:T(256)}, s32[2,16]{1,0:T(2,128)}, f32[3]{0:T(128)}, bf16[12,12288]{1,0:T(8,128)(2,1)}, f32[12,12288]{1,0:T(8,128)}, /*index=5*/bf16[4,16384]{1,0:T(4,128)(2,1)}, ...), branch_computations={%region_0.0_spmd, %region_1.0_spmd} | conditional | bytes 24 | solution.py:575
  4.3 113.3 %routed_exchange.1 = (bf16[1536,768]{1,0:T(8,128)(2,1)S(1)}, bf16[512,1024]{1,0:T(8,128)(2,1)S(1)}, bf16[2,896,2048]{2,1,0:T(8,128)(2,1)S(1)}) custom-call(s32[208]{0:T(256)} %get-tuple-element.58.route_table, s32[2,16]{1,0:T(2,128)} %get-tuple-element.59.slot_table, f32[3]{0:T(128)} %get-tuple-element.60.decay_table, ...), custom_call_target="tpu_custom_call" | custom-call | tf_op jit(solution)/shard_map/cond/branch_1_fun/routed_exchange/pallas_call | solution.py:523
  117.6 4.1 %settle.3 = (bf16[1536,768]{1,0:T(8,128)(2,1)}, bf16[512,1024]{1,0:T(8,128)(2,1)}, bf16[2,896,2048]{2,1,0:T(8,128)(2,1)}) custom-call(bf16[1536,768]{1,0:T(8,128)(2,1)S(1)} %get-tuple-element.67.query_in, bf16[512,1024]{1,0:T(8,128)(2,1)S(1)} %get-tuple-element.68.latent_in, bf16[2,896,2048]{2,1,0:T(8,128)(2,1)S(1)} %get-tuple-element.69.expert_in), custom_call_target="tpu_custom_call" | custom-call | tf_op jit(solution)/shard_map/cond/branch_1_fun/settle/pallas_call | solution.py:565

commit v6 on v5

--- a/solution.py
+++ b/solution.py
@@ -50,14 +50,13 @@
 
     for p in range(HOSTS):
         route[HELD + jnp.clip(expert_of[p], 0, HOSTS - 1)] = p
-        need[0, p] = 0
-        need[1, p] = 0
+        need[p] = 0
     for t in range(HOSTS):
         for s in range(slots_of.shape[0]):
             e = slots_of[s, t]
             p = held_by(e)
-            for h in range(2):
-                need[h, p] = need[h, p] | jnp.where(e >= 0, 1 << ring_place(h, t)[1], 0)
+            bits = sum(1 << (h * SIDE + ring_place(h, t)[1]) for h in range(2))
+            need[p] = need[p] | jnp.where(e >= 0, bits, 0)
 
     good = jnp.bool_(True)
     for h in range(2):
@@ -67,7 +66,7 @@
         wants = []
         for p in range(HOSTS):
             _, v = ring_place(h, p)
-            rows = need[h, p]
+            rows = need[p] >> (h * SIDE)
             near = [(rows >> shifted(v, 1)) & 1, (rows >> shifted(v, 3)) & 1]
             across = (rows >> shifted(v, 2)) & 1
             wants.append((near, across))
@@ -510,7 +509,7 @@
         ),
         in_specs=[smem] * 2,
         out_specs=(smem,) * 2,
-        scratch_shapes=[pltpu.SMEM((2, HOSTS), jnp.int32)],
+        scratch_shapes=[pltpu.SMEM((HOSTS,), jnp.int32)],
     )(shard_expert, host_slots.T)
 
     def exchange(routed, *operands):

time: 122 us -> 122 us (level)
  no operation moved by 1% of the time
where the time goes in v6:
time: 122 us
  Pallas kernels  120 us (98%)
  between operations  1.29 us (1%)
    pallas_call x1, Pallas kernels, exchange(): pl.pallas_call(functools.partial(kernel, routed), name='routed_exchange'...  113 us
    pallas_call x1, Pallas kernels, exchange(): pl.pallas_call(settle, name='settle', out_shape=tuple((jax.ShapeDtypeStru...  4.12 us
    pallas_call x1, Pallas kernels, per_device(): pl.pallas_call(router, name='router', out_shape=(jax.ShapeDtypeStruct((HE...  2.86 us

profile of v6, /device:TPU:0, one launch (start us, length us, event | category | flops | bytes accessed | tf_op | source)
XLA Modules:
  0.0 121.6 jit_solution(9430229938362124536)
XLA Ops:
  0.6 2.9 %router.1 = (s32[208]{0:T(256)}, s32[1]{0:T(128)}) custom-call(s32[16]{0:T(128)} %expert_of.1, s32[2,16]{1,0:T(2,128)} %bitcast.10), custom_call_target="tpu_custom_call" | custom-call | tf_op jit(solution)/shard_map/router/pallas_call | solution.py:503
  4.1 117.5 %conditional.1 = (bf16[1536,768]{1,0:T(8,128)(2,1)}, bf16[512,1024]{1,0:T(8,128)(2,1)}, bf16[1,2,896,2048]{3,2,1,0:T(8,128)(2,1)}) conditional(s32[]{:T(128)} %bitcast.3, (s32[208]{0:T(256)}, s32[2,16]{1,0:T(2,128)}, f32[3]{0:T(128)}, bf16[12,12288]{1,0:T(8,128)(2,1)}, f32[12,12288]{1,0:T(8,128)}, /*index=5*/bf16[4,16384]{1,0:T(4,128)(2,1)}, ...), branch_computations={%region_0.0_spmd, %region_1.0_spmd} | conditional | bytes 24 | solution.py:574
  4.2 113.3 %routed_exchange.1 = (bf16[1536,768]{1,0:T(8,128)(2,1)S(1)}, bf16[512,1024]{1,0:T(8,128)(2,1)S(1)}, bf16[2,896,2048]{2,1,0:T(8,128)(2,1)S(1)}) custom-call(s32[208]{0:T(256)} %get-tuple-element.58.route_table, s32[2,16]{1,0:T(2,128)} %get-tuple-element.59.slot_table, f32[3]{0:T(128)} %get-tuple-element.60.decay_table, ...), custom_call_target="tpu_custom_call" | custom-call | tf_op jit(solution)/shard_map/cond/branch_1_fun/routed_exchange/pallas_call | solution.py:522
  117.5 4.1 %settle.3 = (bf16[1536,768]{1,0:T(8,128)(2,1)}, bf16[512,1024]{1,0:T(8,128)(2,1)}, bf16[2,896,2048]{2,1,0:T(8,128)(2,1)}) custom-call(bf16[1536,768]{1,0:T(8,128)(2,1)S(1)} %get-tuple-element.67.query_in, bf16[512,1024]{1,0:T(8,128)(2,1)S(1)} %get-tuple-element.68.latent_in, bf16[2,896,2048]{2,1,0:T(8,128)(2,1)S(1)} %get-tuple-element.69.expert_in), custom_call_target="tpu_custom_call" | custom-call | tf_op jit(solution)/shard_map/cond/branch_1_fun/settle/pallas_call | solution.py:564
